TPU v7x, 32 devices: a whole 2x2x4 slice. The times are simulated.
32 devices in a mesh: dp: 2 (over core), seqo: 4 (over y, x), seqi: 4 (over z).
Axes of the slice: x: 2, y: 2, z: 4, core: 2. Of those that a mesh axis runs over, the one named last changes fastest.
Arguments:
- loaded: bfloat16 [4096, 1024], P(('dp', 'seqo', 'seqi')), parts along dimension 0, may hold values from -6 to 6
- packing: int32 [8, 4, 4, 2], P(('dp', 'seqo')), parts along dimension 0, may hold values from 0 to 128, as said below
- pattern: int32 [32, 64, 64], P(('dp', 'seqo', 'seqi')), parts along dimension 0, may hold values from 0 to 1, as said below
- w_query: bfloat16 [1024, 1024], replicated, may hold values from -0.1875 to 0.1875
- w_key: bfloat16 [1024, 1024], replicated, may hold values from -0.1875 to 0.1875
- w_value: bfloat16 [1024, 1024], replicated, may hold values from -0.1875 to 0.1875
- norm_gain: float32 [1024], replicated, may hold values from 0.25 to 1.75
- w_out: bfloat16 [1024, 1024], replicated, may hold values from -0.1875 to 0.1875
Outputs:
- mixed: float32 [4096, 1024], P(('dp', 'seqo', 'seqi')), parts along dimension 0
There are 2 independent parts, one for each index of `dp`. A program takes and returns all parts, laid end to end along the dimension named above; an argument that names none is the same for every part. Nothing has to cross between parts.
Inputs may be any that keep to these rules, and one draw needn't show every extreme that they name: `packing`: for each group and source s the counts over d sum to 128 and the offsets are their running sums in the order of d; for each destination d the counts over s sum to 128; a count is at most 64, and some count of every group equals 64. pattern[c, i, j] is 1 where j == i and 0 where j > i.
All inputs are finite; a program needn't handle non-finite values.
Results may differ from a plain program's by a relative error of at most 0.0053.
Values may be sent and summed in bfloat16 or wider, within the bound.
No kernel may reach another device: no remote copies, remote signals or barrier semaphores. Data moves between devices by JAX's collectives and lax.ppermute only.
A program may use at most 128 MiB of HBM per device.

v0:
```python
import functools

import jax
import jax.numpy as jnp
from jax import lax
from jax.experimental import pallas as pl
from jax.experimental.pallas import tpu as pltpu
from jax.sharding import PartitionSpec as P


H = 16
EPSILON = 1e-06
LANES = 256
VMEM = 16 * 2**20


F32 = jnp.float32
BF16 = jnp.bfloat16


def mm(a, b):
    return lax.dot_general(a, b, (((1,), (0,)), ((), ())), preferred_element_type=F32)


def mm_nt(a, b):
    return lax.dot_general(a, b, (((1,), (1,)), ((), ())), preferred_element_type=F32)


def mm_tn(a, b):
    return lax.dot_general(a, b, (((0,), (0,)), ((), ())), preferred_element_type=F32)


def iota(shape, dim):
    return lax.broadcasted_iota(jnp.int32, shape, dim)


def diagonal(blocks, head):
    width = blocks.shape[1]
    heads = width // head
    rows = blocks.shape[0] // heads
    column = iota((rows, width), 1) // head
    out = jnp.zeros((rows, width), blocks.dtype)
    for i in range(heads):
        out = jnp.where(column == i, blocks[i * rows : (i + 1) * rows], out)
    return out


def fetch(pairs, sems):
    copies = [pltpu.make_async_copy(src, dst, sems.at[i]) for i, (src, dst) in enumerate(pairs)]
    for copy in copies:
        copy.start()
    return copies


def state_kernel(head, width, x_hbm, wk_hbm, wv_hbm, s_ref, key_ref, value_ref, x, wk, wv, sems):
    steps = x.shape[1] // width
    pairs = [(x_hbm, x)]
    for j in range(steps):
        cols = pl.ds(j * width, width)
        pairs += [(wk_hbm.at[:, cols], wk.at[:, cols]), (wv_hbm.at[:, cols], wv.at[:, cols])]
    copies = fetch(pairs, sems)
    copies[0].wait()
    rows = x[...]
    for j in range(steps):
        cols = pl.ds(j * width, width)
        copies[1 + 2 * j].wait()
        key = mm(rows, wk[:, cols]).astype(BF16)
        copies[2 + 2 * j].wait()
        value = mm(rows, wv[:, cols]).astype(BF16)
        key_ref[:, cols], value_ref[:, cols] = key, value
        s_ref[:, cols] = diagonal(mm_tn(key, value), head).astype(BF16)


def slot_kernel(axis, table, x_ref, *slot_refs):
    me = lax.axis_index(axis)
    rows, cap = x_ref.shape[0], slot_refs[0].shape[0]
    x = x_ref[...]
    slot, row = iota((cap, rows), 0), iota((cap, rows), 1)
    for k, slot_ref in enumerate(slot_refs, 1):
        first, count = table[0, me, 0, me ^ k], table[0, me, 1, me ^ k]
        pick = jnp.logical_and(row == first + slot, slot < count)
        slot_ref[...] = mm(pick.astype(BF16), x).astype(BF16)


def bound_kernel(axis, head, width, table, key_ref, value_ref, *m_refs):
    me = lax.axis_index(axis)
    rows, depth = key_ref.shape
    row = iota((rows, width), 0)
    for j in range(depth // width):
        cols = pl.ds(j * width, width)
        key, value = key_ref[:, cols], value_ref[:, cols]
        for k, m_ref in enumerate(m_refs):
            kept = jnp.where(row < table[0, me, 0, me ^ k], value, jnp.zeros_like(value))
            m_ref[:, cols] = diagonal(mm_tn(key, kept), head)


def local_kernel(axis, head, width, table, pattern_ref, x_ref, wq_hbm, wk_hbm, wv_hbm, *rest):
    slots, (q_ref, local_ref, wq, wk, wv, sems) = rest[:-6], rest[-6:]
    rows, depth = x_ref.shape
    n, steps = len(slots) + 1, depth // width
    pairs = []
    for j in range(steps):
        cols = pl.ds(j * width, width)
        for src, dst in ((wq_hbm, wq), (wk_hbm, wk), (wv_hbm, wv)):
            pairs.append((src.at[:, cols], dst.at[:, cols]))
    copies = fetch(pairs, sems)
    me = lax.axis_index(axis)
    total = None
    for k in range(n):
        source = me ^ k
        start = jnp.int32(0)
        for s in range(n):
            start += jnp.where(s < source, table[0, s, 1, me], 0)
        count = table[0, source, 1, me]
        held = x_ref[...] if k == 0 else slots[k - 1][...]
        first = table[0, me, 0, me] if k == 0 else 0
        row, slot = iota((rows, held.shape[0]), 0), iota((rows, held.shape[0]), 1)
        place = row - start
        pick = (slot == place + first) & (place >= 0) & (place < count)
        part = mm(pick.astype(BF16), held)
        total = part if total is None else total + part
    x = total.astype(BF16)
    frames = pattern_ref.shape[1]
    per = rows // frames
    grow = (iota((rows, frames), 0) // per == iota((rows, frames), 1)).astype(BF16)
    seen = (pattern_ref[0] > 0).astype(BF16)
    allowed = mm_nt(mm(grow, seen).astype(BF16), grow) > 0.5
    heads = width // head
    column = iota((rows, width), 1) // head
    for j in range(steps):
        cols = pl.ds(j * width, width)
        copies[3 * j].wait()
        query = mm(x, wq[:, cols]).astype(BF16)
        copies[3 * j + 1].wait()
        key = mm(x, wk[:, cols]).astype(BF16)
        copies[3 * j + 2].wait()
        value = mm(x, wv[:, cols]).astype(BF16)
        zero = jnp.zeros_like(query)
        stacked = jnp.concatenate([jnp.where(column == i, query, zero) for i in range(heads)], axis=0)
        scores = mm_nt(stacked, key)
        masked = jnp.concatenate(
            [jnp.where(allowed, scores[i * rows : (i + 1) * rows], 0.0) for i in range(heads)], axis=0
        ).astype(BF16)
        local_ref[:, cols] = diagonal(mm(masked, value), head)
        q_ref[:, cols] = query


def out_kernel(head, width, q_ref, local_ref, kept_ref, recv_ref, gain_ref, w_hbm, out_ref, w, sems):
    _, depth = q_ref.shape
    steps = depth // width
    pairs = []
    for j in range(steps):
        part = pl.ds(j * width, width)
        pairs.append((w_hbm.at[part], w.at[part]))
    copies = fetch(pairs, sems)
    heads = width // head
    same = iota((width, width), 0) // head == iota((width, width), 1) // head
    ones = same.astype(BF16)
    zero = jnp.zeros((width, width), BF16)
    total = None
    for j in range(steps):
        cols = pl.ds(j * width, width)
        prefix = kept_ref[:, cols] + recv_ref[:, cols].astype(F32)
        high = prefix.astype(BF16)
        low = (prefix - high.astype(F32)).astype(BF16)
        query = q_ref[:, cols]
        attended = local_ref[:, cols]
        for part in (high, low):
            spread = jnp.where(same, jnp.concatenate([part] * heads, axis=0), zero)
            attended = attended + mm(query, spread)
        square = attended * attended
        sq_high = square.astype(BF16)
        sq_low = (square - sq_high.astype(F32)).astype(BF16)
        mean = (mm(sq_high, ones) + mm(sq_low, ones)) * (1.0 / head)
        normed = (attended * lax.rsqrt(mean + EPSILON) * gain_ref[:, cols]).astype(BF16)
        copies[j].wait()
        piece = mm(normed, w[pl.ds(j * width, width), :])
        total = piece if total is None else total + piece
    out_ref[...] = total


def swap(value, axis, bits):
    return lax.ppermute(value, axis, [(i, i ^ bits) for i in range(lax.axis_size(axis))])


def earlier_groups(state, axis):
    count, mine = lax.axis_size(axis), lax.axis_index(axis)
    before, total, stride = None, state, 1
    while stride < count:
        radix = min(4, count // stride)
        digit = (mine // stride) % radix
        came = [swap(total.astype(BF16), axis, k * stride).astype(F32) for k in range(1, radix)]
        for k, piece in enumerate(came, 1):
            piece_before = jnp.where((digit ^ k) < digit, piece, 0.0)
            before = piece_before if before is None else before + piece_before
        stride *= radix
        if stride < count:
            total = total.astype(F32) + sum(came)
    return before


def cost(flops, size):
    return pl.CostEstimate(flops=flops, bytes_accessed=size, transcendentals=0)


def body(loaded, packing, pattern, w_query, w_key, w_value, norm_gain, w_out):
    n = lax.axis_size("seqi")
    rows, depth = loaded.shape
    head = depth // H
    width = min(LANES, depth)
    steps = depth // width
    cap = 2 * rows // n
    square = depth * depth
    table = jnp.swapaxes(packing, 2, 3)
    smem = pl.BlockSpec(memory_space=pltpu.SMEM)
    vmem = pl.BlockSpec(memory_space=pltpu.VMEM)
    hbm = pl.BlockSpec(memory_space=pltpu.HBM)
    shape = jax.ShapeDtypeStruct
    weight = pltpu.VMEM((depth, depth), BF16)
    params = pltpu.CompilerParams(vmem_limit_bytes=VMEM)

    state, key, value = pl.pallas_call(
        functools.partial(state_kernel, head, width),
        in_specs=[hbm] * 3,
        out_specs=[vmem] * 3,
        out_shape=[shape((head, depth), BF16)] + [shape((rows, depth), BF16)] * 2,
        scratch_shapes=[pltpu.VMEM((rows, depth), BF16), weight, weight]
        + [pltpu.SemaphoreType.DMA((1 + 2 * steps,))],
        cost_estimate=cost(4 * rows * square, 4 * square),
        name="states",
    )(loaded, w_key, w_value)
    before = earlier_groups(state, "seqo")
    slots = pl.pallas_call(
        functools.partial(slot_kernel, "seqi"),
        in_specs=[smem, vmem],
        out_specs=[vmem] * (n - 1),
        out_shape=[shape((cap, depth), BF16)] * (n - 1),
        compiler_params=params,
        cost_estimate=cost(4 * rows * rows * depth, 4 * rows * depth),
        name="slots",
    )(table, loaded)
    came = [swap(slots[k - 1], "seqi", k) for k in range(1, n)]
    bound = pl.pallas_call(
        functools.partial(bound_kernel, "seqi", head, width),
        in_specs=[smem, vmem, vmem],
        out_specs=[vmem] * n,
        out_shape=[shape((head, depth), F32)] * n,
        compiler_params=params,
        cost_estimate=cost(2 * n * rows * head * depth * 4, 4 * rows * depth),
        name="bounds",
    )(table, key, value)

    held = {k: bound[k] if before is None else before + bound[k] for k in range(n)}
    bit = 1
    while bit < n:
        send = [k for k in held if k & bit]
        if len(send) > 1:
            got = swap(jnp.stack([held[k].astype(BF16) for k in send]), "seqi", bit)
        else:
            got = [swap(held[send[0]].astype(BF16), "seqi", bit)]
        if 2 * bit < n:
            held = {k ^ bit: held[k ^ bit] + got[i].astype(F32) for i, k in enumerate(send)}
        else:
            last = got[0]
        bit *= 2

    query, local = pl.pallas_call(
        functools.partial(local_kernel, "seqi", head, width),
        in_specs=[smem, vmem, vmem] + [hbm] * 3 + [vmem] * (n - 1),
        out_specs=[vmem] * 2,
        out_shape=[shape((rows, depth), BF16), shape((rows, depth), F32)],
        scratch_shapes=[weight] * 3 + [pltpu.SemaphoreType.DMA((3 * steps,))],
        compiler_params=params,
        cost_estimate=cost(6 * rows * square, 6 * square),
        name="local",
    )(table, pattern, loaded, w_query, w_key, w_value, *came)

    return pl.pallas_call(
        functools.partial(out_kernel, head, width),
        in_specs=[vmem] * 5 + [hbm],
        out_specs=vmem,
        out_shape=shape((rows, depth), F32),
        scratch_shapes=[weight, pltpu.SemaphoreType.DMA((steps,))],
        compiler_params=params,
        cost_estimate=cost(2 * rows * square, 2 * square),
        name="out",
    )(query, local, held[0], last, norm_gain.reshape(1, depth), w_out)


def solution(mesh):
    return jax.shard_map(
        body,
        mesh=mesh,
        in_specs=(
            P(("dp", "seqo", "seqi"), None),
            P(("dp", "seqo"), None, None, None),
            P(("dp", "seqo", "seqi"), None, None),
            P(),
            P(),
            P(),
            P(),
            P(),
        ),
        out_specs=P(("dp", "seqo", "seqi"), None),
        check_vma=False,
    )
```

profile of v0, /device:TPU:0, one launch (start us, length us, event | category | flops | bytes accessed | tf_op | source)
XLA Modules:
  0.0 44.8 jit_solution(13579940475552858412)
XLA Ops:
  0.0 0.0 copy-start.6
  0.0 0.0 copy-start.3
  0.0 5.1 %states.1 = (bf16[64,1024]{1,0:T(8,128)(2,1)}, bf16[128,1024]{1,0:T(8,128)(2,1)}, bf16[128,1024]{1,0:T(8,128)(2,1)}) custom-call(bf16[128,1024]{1,0:T(8,128)(2,1)} %x_hbm.1, bf16[1024,1024]{1,0:T(8,128)(2,1)} %wk_hbm.3, bf16[1024,1024]{1,0:T(8,128)(2,1)} %wv_hbm.3), custom_call_target="tpu_custom_call" | custom-call | flops 536870912 | bytes 4194304 | tf_op jit(solution)/shard_map/states/pallas_call | solution.py:222
  5.1 0.0 copy-start.2
  5.1 3.0 %collective-permute-start.3 = (bf16[64,1024]{1,0:T(8,128)(2,1)}, bf16[64,1024]{1,0:T(8,128)(2,1)S(1)}, u32[]{:S(2)}, u32[]{:S(2)}) collective-permute-start(bf16[64,1024]{1,0:T(8,128)(2,1)} %get-tuple-element.22), channel_id=1, source_target_pairs={{0,4},{4,0},{8,12},{12,8},{1,5},{5,1},{9,13},{13,9},{2,6},{6,2},{1... | collective-permute-start | bytes 393224 | tf_op jit(solution)/shard_map/ppermute | solution.py:183
  8.1 1.5 %collective-permute-start.4 = (bf16[64,1024]{1,0:T(8,128)(2,1)}, bf16[64,1024]{1,0:T(8,128)(2,1)S(1)}, u32[]{:S(2)}, u32[]{:S(2)}) collective-permute-start(bf16[64,1024]{1,0:T(8,128)(2,1)} %get-tuple-element.22), channel_id=1, source_target_pairs={{0,8},{4,12},{8,0},{12,4},{1,9},{5,13},{9,1},{13,5},{2,10},{6,14},... | collective-permute-start | bytes 393224 | tf_op jit(solution)/shard_map/ppermute | solution.py:183
  9.7 0.0 collective-permute-start.5
  9.7 0.0 copy-done.6
  9.7 0.0 copy-start.8
  9.7 0.9 %copy-done.8 = bf16[128,1024]{1,0:T(8,128)(2,1)S(1)} copy-done((bf16[128,1024]{1,0:T(8,128)(2,1)S(1)}, bf16[128,1024]{1,0:T(8,128)(2,1)}, u32[]{:S(2)}) %copy-start.8) | copy-done | bytes 262168
  10.6 0.0 copy-start.9
  10.6 0.9 %copy-done.9 = bf16[128,1024]{1,0:T(8,128)(2,1)S(1)} copy-done((bf16[128,1024]{1,0:T(8,128)(2,1)S(1)}, bf16[128,1024]{1,0:T(8,128)(2,1)}, u32[]{:S(2)}) %copy-start.9) | copy-done | bytes 262168
  11.6 0.0 copy-start
  11.6 0.0 copy-start.1
  11.6 0.0 copy-start.5
  11.6 1.3 %bounds.1 = (f32[64,1024]{1,0:T(8,128)S(1)}, f32[64,1024]{1,0:T(8,128)S(1)}, f32[64,1024]{1,0:T(8,128)S(1)}, f32[64,1024]{1,0:T(8,128)S(1)}) custom-call(s32[1,4,2,4]{3,2,1,0:T(2,128)S(1)} %bitcast.16, bf16[128,1024]{1,0:T(8,128)(2,1)S(1)} %copy-done.8, bf16[128,1024]{1,0:T(8,128)(2,1)S(1)} %copy-done.9), custom_call_target="tpu_custom_call" | custom-call | flops 268435456 | bytes 524288 | tf_op jit(solution)/shard_map/bounds/pallas_call | solution.py:243
  12.9 0.0 collective-permute-done.3
  12.9 3.2 %collective-permute-done.4 = bf16[64,1024]{1,0:T(8,128)(2,1)S(1)} collective-permute-done((bf16[64,1024]{1,0:T(8,128)(2,1)}, bf16[64,1024]{1,0:T(8,128)(2,1)S(1)}, u32[]{:S(2)}, u32[]{:S(2)}) %collective-permute-start.4) | collective-permute-done | bytes 131104 | tf_op jit(solution)/shard_map/ppermute | solution.py:183
  16.1 0.0 collective-permute-done.5
  16.1 0.1 fusion.1
  16.3 1.6 %collective-permute-start.6 = (bf16[2,64,1024]{2,1,0:T(8,128)(2,1)S(1)}, bf16[2,64,1024]{2,1,0:T(8,128)(2,1)S(1)}, u32[]{:S(2)}, u32[]{:S(2)}) collective-permute-start(bf16[2,64,1024]{2,1,0:T(8,128)(2,1)S(1)} %pad_maximum_fusion), channel_id=1, source_target_pairs={{0,1},{1,0},{2,3},{3,2},{4,5},{5,4},{6,7},{7,6},{8,9},{9,8},{10,11... | collective-permute-start | bytes 786440 | tf_op jit(solution)/shard_map/ppermute | solution.py:183
  17.9 0.0 copy-done.2
  17.9 0.9 %slots.1 = (bf16[64,1024]{1,0:T(8,128)(2,1)S(1)}, bf16[64,1024]{1,0:T(8,128)(2,1)S(1)}, bf16[64,1024]{1,0:T(8,128)(2,1)S(1)}) custom-call(s32[1,4,2,4]{3,2,1,0:T(2,128)S(1)} %bitcast.17, bf16[128,1024]{1,0:T(8,128)(2,1)S(1)} %copy-done.2), custom_call_target="tpu_custom_call" | custom-call | flops 67108864 | bytes 524288 | tf_op jit(solution)/shard_map/slots/pallas_call | solution.py:233
  18.8 0.5 %collective-permute-start = (bf16[64,1024]{1,0:T(8,128)(2,1)S(1)}, bf16[64,1024]{1,0:T(8,128)(2,1)S(1)}, u32[]{:S(2)}, u32[]{:S(2)}) collective-permute-start(bf16[64,1024]{1,0:T(8,128)(2,1)S(1)} %get-tuple-element.17), channel_id=1, source_target_pairs={{0,1},{1,0},{2,3},{3,2},{4,5},{5,4},{6,7},{7,6},{8,9},{9,8},{10,11... | collective-permute-start | bytes 393224 | tf_op jit(solution)/shard_map/ppermute | solution.py:183
  19.3 2.6 %collective-permute-start.1 = (bf16[64,1024]{1,0:T(8,128)(2,1)S(1)}, bf16[64,1024]{1,0:T(8,128)(2,1)S(1)}, u32[]{:S(2)}, u32[]{:S(2)}) collective-permute-start(bf16[64,1024]{1,0:T(8,128)(2,1)S(1)} %get-tuple-element.18), channel_id=1, source_target_pairs={{0,2},{1,3},{2,0},{3,1},{4,6},{5,7},{6,4},{7,5},{8,10},{9,11},{10,... | collective-permute-start | bytes 393224 | tf_op jit(solution)/shard_map/ppermute | solution.py:183
  21.9 1.3 %collective-permute-start.2 = (bf16[64,1024]{1,0:T(8,128)(2,1)S(1)}, bf16[64,1024]{1,0:T(8,128)(2,1)S(1)}, u32[]{:S(2)}, u32[]{:S(2)}) collective-permute-start(bf16[64,1024]{1,0:T(8,128)(2,1)S(1)} %get-tuple-element.19), channel_id=1, source_target_pairs={{0,3},{1,2},{2,1},{3,0},{4,7},{5,6},{6,5},{7,4},{8,11},{9,10},{10,... | collective-permute-start | bytes 393224 | tf_op jit(solution)/shard_map/ppermute | solution.py:183
  23.2 4.7 %collective-permute-done.6 = bf16[2,64,1024]{2,1,0:T(8,128)(2,1)S(1)} collective-permute-done((bf16[2,64,1024]{2,1,0:T(8,128)(2,1)S(1)}, bf16[2,64,1024]{2,1,0:T(8,128)(2,1)S(1)}, u32[]{:S(2)}, u32[]{:S(2)}) %collective-permute-start.6) | collective-permute-done | bytes 262176 | tf_op jit(solution)/shard_map/ppermute | solution.py:183
  28.0 0.1 fusion
  28.1 0.0 copy-start.4
  28.1 0.0 copy-start.7
  28.1 3.2 %collective-permute-start.7 = (bf16[64,1024]{1,0:T(8,128)(2,1)S(1)}, bf16[64,1024]{1,0:T(8,128)(2,1)S(1)}, u32[]{:S(2)}, u32[]{:S(2)}) collective-permute-start(bf16[64,1024]{1,0:T(8,128)(2,1)S(1)} %get-tuple-element.29), channel_id=1, source_target_pairs={{0,2},{1,3},{2,0},{3,1},{4,6},{5,7},{6,4},{7,5},{8,10},{9,11},{10,... | collective-permute-start | bytes 393224 | tf_op jit(solution)/shard_map/ppermute | solution.py:183
  31.3 0.1 collective-permute-done.rest_0_
  31.4 0.0 collective-permute-done.1.rest_1_
  31.4 3.7 %collective-permute-done.2.rest_2_ = bf16[64,1024]{1,0:T(8,128)(2,1)S(1)} collective-permute-done((bf16[64,1024]{1,0:T(8,128)(2,1)S(1)}, bf16[64,1024]{1,0:T(8,128)(2,1)S(1)}, u32[]{:S(2)}, u32[]{:S(2)}) %collective-permute-start.2) | collective-permute-done | bytes 131104 | tf_op jit(solution)/shard_map/ppermute | solution.py:183
  35.1 0.0 copy-done.3
  35.1 0.0 copy-done
  35.1 0.0 copy-done.1
  35.1 0.0 copy-done.5
  35.1 6.6 %local.1 = (bf16[128,1024]{1,0:T(8,128)(2,1)S(1)}, f32[128,1024]{1,0:T(8,128)S(1)}) custom-call(s32[1,4,2,4]{3,2,1,0:T(2,128)S(1)} %bitcast.18, s32[1,64,64]{2,1,0:T(8,128)S(1)} %copy-done.5, bf16[128,1024]{1,0:T(8,128)(2,1)S(1)} %copy-done.2, bf16[1024,1024]{1,0:T(8,128)(2,1)S(1)} %copy-done.3, bf16[1024,1024]{1,0:T(8,128)(2,1)S(1)} %copy-done, ...), custom_call_target="tpu_custom_call" | custom-call | flops 805306368 | bytes 6291456 | tf_op jit(solution)/shard_map/local/pallas_call | solution.py:267
  41.8 0.0 collective-permute-done.7.recv_ref
  41.8 0.0 copy-done.4
  41.8 0.0 copy-done.7
  41.8 3.0 %out.1 = f32[128,1024]{1,0:T(8,128)} custom-call(bf16[128,1024]{1,0:T(8,128)(2,1)S(1)} %get-tuple-element.20.q_ref, f32[128,1024]{1,0:T(8,128)S(1)} %get-tuple-element.21.local_ref, f32[64,1024]{1,0:T(8,128)S(1)} %get-tuple-element.30.kept_ref, bf16[64,1024]{1,0:T(8,128)(2,1)S(1)} %collective-permute-done.7.recv_ref, f32[1,1024]{1,0:T(1,128)S(1)} %bitcast.19, ...), custom_call_target="tpu_custom_call" | custom-call | flops 268435456 | bytes 2097152 | tf_op jit(solution)/shard_map/out/pallas_call | solution.py:278
  (1 shorter events, 0.0 us)
Async XLA Ops:
  0.0 9.7 %copy-start.6 = (s32[1,4,4,2]{2,3,1,0:T(2,128)S(1)}, s32[1,4,4,2]{2,3,1,0:T(2,128)}, u32[]{:S(2)}) copy-start(s32[1,4,4,2]{2,3,1,0:T(2,128)} %param.9) | copy-start | bytes 388
  0.0 35.1 %copy-start.3 = (bf16[1024,1024]{1,0:T(8,128)(2,1)S(1)}, bf16[1024,1024]{1,0:T(8,128)(2,1)}, u32[]{:S(2)}) copy-start(bf16[1024,1024]{1,0:T(8,128)(2,1)} %wq_hbm.1) | copy-start | bytes 6291460
  5.1 12.8 %copy-start.2 = (bf16[128,1024]{1,0:T(8,128)(2,1)S(1)}, bf16[128,1024]{1,0:T(8,128)(2,1)}, u32[]{:S(2)}) copy-start(bf16[128,1024]{1,0:T(8,128)(2,1)} %x_hbm.1) | copy-start | bytes 786436
  5.1 7.8 %collective-permute-start.3 = (bf16[64,1024]{1,0:T(8,128)(2,1)}, bf16[64,1024]{1,0:T(8,128)(2,1)S(1)}, u32[]{:S(2)}, u32[]{:S(2)}) collective-permute-start(bf16[64,1024]{1,0:T(8,128)(2,1)} %get-tuple-element.22), channel_id=1, source_target_pairs={{0,4},{4,0},{8,12},{12,8},{1,5},{5,1},{9,13},{13,9},{2,6},{6,2},{1... | collective-permute-start | bytes 393224 | tf_op jit(solution)/shard_map/ppermute | solution.py:183
  8.1 8.0 %collective-permute-start.4 = (bf16[64,1024]{1,0:T(8,128)(2,1)}, bf16[64,1024]{1,0:T(8,128)(2,1)S(1)}, u32[]{:S(2)}, u32[]{:S(2)}) collective-permute-start(bf16[64,1024]{1,0:T(8,128)(2,1)} %get-tuple-element.22), channel_id=1, source_target_pairs={{0,8},{4,12},{8,0},{12,4},{1,9},{5,13},{9,1},{13,5},{2,10},{6,14},... | collective-permute-start | bytes 393224 | tf_op jit(solution)/shard_map/ppermute | solution.py:183
  9.7 6.5 %collective-permute-start.5 = (bf16[64,1024]{1,0:T(8,128)(2,1)}, bf16[64,1024]{1,0:T(8,128)(2,1)S(1)}, u32[]{:S(2)}, u32[]{:S(2)}) collective-permute-start(bf16[64,1024]{1,0:T(8,128)(2,1)} %get-tuple-element.22), channel_id=1, source_target_pairs={{0,12},{4,8},{8,4},{12,0},{1,13},{5,9},{9,5},{13,1},{2,14},{6,10},... | collective-permute-start | bytes 393224 | tf_op jit(solution)/shard_map/ppermute | solution.py:183
  9.7 1.0 %copy-start.8 = (bf16[128,1024]{1,0:T(8,128)(2,1)S(1)}, bf16[128,1024]{1,0:T(8,128)(2,1)}, u32[]{:S(2)}) copy-start(bf16[128,1024]{1,0:T(8,128)(2,1)} %get-tuple-element.23.key_ref) | copy-start | bytes 786436
  10.6 0.9 %copy-start.9 = (bf16[128,1024]{1,0:T(8,128)(2,1)S(1)}, bf16[128,1024]{1,0:T(8,128)(2,1)}, u32[]{:S(2)}) copy-start(bf16[128,1024]{1,0:T(8,128)(2,1)} %get-tuple-element.24.value_ref) | copy-start | bytes 786436
  11.6 23.5 %copy-start = (bf16[1024,1024]{1,0:T(8,128)(2,1)S(1)}, bf16[1024,1024]{1,0:T(8,128)(2,1)}, u32[]{:S(2)}) copy-start(bf16[1024,1024]{1,0:T(8,128)(2,1)} %wk_hbm.3) | copy-start | bytes 6291460
  11.6 23.5 %copy-start.1 = (bf16[1024,1024]{1,0:T(8,128)(2,1)S(1)}, bf16[1024,1024]{1,0:T(8,128)(2,1)}, u32[]{:S(2)}) copy-start(bf16[1024,1024]{1,0:T(8,128)(2,1)} %wv_hbm.3) | copy-start | bytes 6291460
  11.6 23.5 %copy-start.5 = (s32[1,64,64]{2,1,0:T(8,128)S(1)}, s32[1,64,64]{2,1,0:T(8,128)}, u32[]{:S(2)}) copy-start(s32[1,64,64]{2,1,0:T(8,128)} %pattern_ref.1) | copy-start | bytes 49156
  16.3 11.7 %collective-permute-start.6 = (bf16[2,64,1024]{2,1,0:T(8,128)(2,1)S(1)}, bf16[2,64,1024]{2,1,0:T(8,128)(2,1)S(1)}, u32[]{:S(2)}, u32[]{:S(2)}) collective-permute-start(bf16[2,64,1024]{2,1,0:T(8,128)(2,1)S(1)} %pad_maximum_fusion), channel_id=1, source_target_pairs={{0,1},{1,0},{2,3},{3,2},{4,5},{5,4},{6,7},{7,6},{8,9},{9,8},{10,11... | collective-permute-start | bytes 786440 | tf_op jit(solution)/shard_map/ppermute | solution.py:183
  18.8 12.6 %collective-permute-start = (bf16[64,1024]{1,0:T(8,128)(2,1)S(1)}, bf16[64,1024]{1,0:T(8,128)(2,1)S(1)}, u32[]{:S(2)}, u32[]{:S(2)}) collective-permute-start(bf16[64,1024]{1,0:T(8,128)(2,1)S(1)} %get-tuple-element.17), channel_id=1, source_target_pairs={{0,1},{1,0},{2,3},{3,2},{4,5},{5,4},{6,7},{7,6},{8,9},{9,8},{10,11... | collective-permute-start | bytes 393224 | tf_op jit(solution)/shard_map/ppermute | solution.py:183
  19.3 12.1 %collective-permute-start.1 = (bf16[64,1024]{1,0:T(8,128)(2,1)S(1)}, bf16[64,1024]{1,0:T(8,128)(2,1)S(1)}, u32[]{:S(2)}, u32[]{:S(2)}) collective-permute-start(bf16[64,1024]{1,0:T(8,128)(2,1)S(1)} %get-tuple-element.18), channel_id=1, source_target_pairs={{0,2},{1,3},{2,0},{3,1},{4,6},{5,7},{6,4},{7,5},{8,10},{9,11},{10,... | collective-permute-start | bytes 393224 | tf_op jit(solution)/shard_map/ppermute | solution.py:183
  21.9 13.2 %collective-permute-start.2 = (bf16[64,1024]{1,0:T(8,128)(2,1)S(1)}, bf16[64,1024]{1,0:T(8,128)(2,1)S(1)}, u32[]{:S(2)}, u32[]{:S(2)}) collective-permute-start(bf16[64,1024]{1,0:T(8,128)(2,1)S(1)} %get-tuple-element.19), channel_id=1, source_target_pairs={{0,3},{1,2},{2,1},{3,0},{4,7},{5,6},{6,5},{7,4},{8,11},{9,10},{10,... | collective-permute-start | bytes 393224 | tf_op jit(solution)/shard_map/ppermute | solution.py:183
  28.1 13.7 %copy-start.4 = (bf16[1024,1024]{1,0:T(8,128)(2,1)S(1)}, bf16[1024,1024]{1,0:T(8,128)(2,1)}, u32[]{:S(2)}) copy-start(bf16[1024,1024]{1,0:T(8,128)(2,1)} %w_hbm.1) | copy-start | bytes 6291460
  28.1 13.7 %copy-start.7 = (f32[1024]{0:T(1024)S(1)}, f32[1024]{0:T(1024)}, u32[]{:S(2)}) copy-start(f32[1024]{0:T(1024)} %param.14) | copy-start | bytes 12292
  28.1 13.6 %collective-permute-start.7 = (bf16[64,1024]{1,0:T(8,128)(2,1)S(1)}, bf16[64,1024]{1,0:T(8,128)(2,1)S(1)}, u32[]{:S(2)}, u32[]{:S(2)}) collective-permute-start(bf16[64,1024]{1,0:T(8,128)(2,1)S(1)} %get-tuple-element.29), channel_id=1, source_target_pairs={{0,2},{1,3},{2,0},{3,1},{4,6},{5,7},{6,4},{7,5},{8,10},{9,11},{10,... | collective-permute-start | bytes 393224 | tf_op jit(solution)/shard_map/ppermute | solution.py:183
where the time goes:
time: 45 us; the launch traced here: 44.8 us
  Pallas kernels  16.9 us (38%)
  starting transfers between devices  13.8 us (31%)
  waiting for transfers between devices  11.7 us (26%)
  local copies, waits for them, and re-layouts  1.94 us (4%)
    ppermute x8, starting transfers between devices, swap(): lax.ppermute(value, axis, [(i, i ^ bits) for i in range(lax.axis_size(axi...  13.8 us
    ppermute x8, waiting for transfers between devices, swap(): lax.ppermute(value, axis, [(i, i ^ bits) for i in range(lax.axis_size(axi...  11.7 us
    pallas_call x1, Pallas kernels, body(): pl.pallas_call(functools.partial(local_kernel, 'seqi', head, width), in_s...  6.63 us
    pallas_call x1, Pallas kernels, body(): pl.pallas_call(functools.partial(state_kernel, head, width), in_specs=[hb...  5.08 us
    pallas_call x1, Pallas kernels, body(): pl.pallas_call(functools.partial(out_kernel, head, width), in_specs=[vmem...  3.02 us
    unnamed x20, local copies, waits for them, and re-layouts  1.94 us
    pallas_call x1, Pallas kernels, body(): pl.pallas_call(functools.partial(bound_kernel, 'seqi', head, width), in_s...  1.34 us
  transfers between devices with their start and end apart: 8, of which 4 were waited for; matrix products, arithmetic and copies ran while one was open for 0% of the time, Pallas kernels for 20%

commit v1 on v0

--- a/solution.py
+++ b/solution.py
@@ -12,6 +12,8 @@
 EPSILON = 1e-06
 LANES = 256
 VMEM = 16 * 2**20
+SLOTS_COST = 10**11
+CHUNKS = 2
 
 
 F32 = jnp.float32
@@ -45,27 +47,11 @@
     return out
 
 
-def fetch(pairs, sems):
-    copies = [pltpu.make_async_copy(src, dst, sems.at[i]) for i, (src, dst) in enumerate(pairs)]
-    for copy in copies:
-        copy.start()
-    return copies
-
-
-def state_kernel(head, width, x_hbm, wk_hbm, wv_hbm, s_ref, key_ref, value_ref, x, wk, wv, sems):
-    steps = x.shape[1] // width
-    pairs = [(x_hbm, x)]
-    for j in range(steps):
+def state_kernel(head, width, x_ref, wk, wv, s_ref, key_ref, value_ref):
+    rows = x_ref[...]
+    for j in range(rows.shape[1] // width):
         cols = pl.ds(j * width, width)
-        pairs += [(wk_hbm.at[:, cols], wk.at[:, cols]), (wv_hbm.at[:, cols], wv.at[:, cols])]
-    copies = fetch(pairs, sems)
-    copies[0].wait()
-    rows = x[...]
-    for j in range(steps):
-        cols = pl.ds(j * width, width)
-        copies[1 + 2 * j].wait()
         key = mm(rows, wk[:, cols]).astype(BF16)
-        copies[2 + 2 * j].wait()
         value = mm(rows, wv[:, cols]).astype(BF16)
         key_ref[:, cols], value_ref[:, cols] = key, value
         s_ref[:, cols] = diagonal(mm_tn(key, value), head).astype(BF16)
@@ -94,16 +80,10 @@
             m_ref[:, cols] = diagonal(mm_tn(key, kept), head)
 
 
-def local_kernel(axis, head, width, table, pattern_ref, x_ref, wq_hbm, wk_hbm, wv_hbm, *rest):
-    slots, (q_ref, local_ref, wq, wk, wv, sems) = rest[:-6], rest[-6:]
+def local_kernel(axis, head, width, table, pattern_ref, x_ref, wq, wk, wv, *rest):
+    slots, (q_ref, local_ref) = rest[:-2], rest[-2:]
     rows, depth = x_ref.shape
     n, steps = len(slots) + 1, depth // width
-    pairs = []
-    for j in range(steps):
-        cols = pl.ds(j * width, width)
-        for src, dst in ((wq_hbm, wq), (wk_hbm, wk), (wv_hbm, wv)):
-            pairs.append((src.at[:, cols], dst.at[:, cols]))
-    copies = fetch(pairs, sems)
     me = lax.axis_index(axis)
     total = None
     for k in range(n):
@@ -129,11 +109,8 @@
     column = iota((rows, width), 1) // head
     for j in range(steps):
         cols = pl.ds(j * width, width)
-        copies[3 * j].wait()
         query = mm(x, wq[:, cols]).astype(BF16)
-        copies[3 * j + 1].wait()
         key = mm(x, wk[:, cols]).astype(BF16)
-        copies[3 * j + 2].wait()
         value = mm(x, wv[:, cols]).astype(BF16)
         zero = jnp.zeros_like(query)
         stacked = jnp.concatenate([jnp.where(column == i, query, zero) for i in range(heads)], axis=0)
@@ -145,14 +122,10 @@
         q_ref[:, cols] = query
 
 
-def out_kernel(head, width, q_ref, local_ref, kept_ref, recv_ref, gain_ref, w_hbm, out_ref, w, sems):
+def out_kernel(head, width, q_ref, local_ref, *rest):
+    kept_refs, recv_refs, (gain_ref, w, out_ref) = rest[:CHUNKS], rest[CHUNKS:-3], rest[-3:]
     _, depth = q_ref.shape
     steps = depth // width
-    pairs = []
-    for j in range(steps):
-        part = pl.ds(j * width, width)
-        pairs.append((w_hbm.at[part], w.at[part]))
-    copies = fetch(pairs, sems)
     heads = width // head
     same = iota((width, width), 0) // head == iota((width, width), 1) // head
     ones = same.astype(BF16)
@@ -160,7 +133,9 @@
     total = None
     for j in range(steps):
         cols = pl.ds(j * width, width)
-        prefix = kept_ref[:, cols] + recv_ref[:, cols].astype(F32)
+        chunk, place = divmod(j * width, depth // CHUNKS)
+        inner = pl.ds(place, width)
+        prefix = kept_refs[chunk][:, inner] + recv_refs[chunk][:, inner].astype(F32)
         high = prefix.astype(BF16)
         low = (prefix - high.astype(F32)).astype(BF16)
         query = q_ref[:, cols]
@@ -173,7 +148,6 @@
         sq_low = (square - sq_high.astype(F32)).astype(BF16)
         mean = (mm(sq_high, ones) + mm(sq_low, ones)) * (1.0 / head)
         normed = (attended * lax.rsqrt(mean + EPSILON) * gain_ref[:, cols]).astype(BF16)
-        copies[j].wait()
         piece = mm(normed, w[pl.ds(j * width, width), :])
         total = piece if total is None else total + piece
     out_ref[...] = total
@@ -186,17 +160,53 @@
 def earlier_groups(state, axis):
     count, mine = lax.axis_size(axis), lax.axis_index(axis)
     before, total, stride = None, state, 1
-    while stride < count:
+    while True:
         radix = min(4, count // stride)
+        came = [swap(total.astype(BF16), axis, k * stride) for k in range(1, radix)]
+        if stride * radix >= count:
+            return before, came, stride
         digit = (mine // stride) % radix
-        came = [swap(total.astype(BF16), axis, k * stride).astype(F32) for k in range(1, radix)]
-        for k, piece in enumerate(came, 1):
+        wide = [piece.astype(F32) for piece in came]
+        for k, piece in enumerate(wide, 1):
             piece_before = jnp.where((digit ^ k) < digit, piece, 0.0)
             before = piece_before if before is None else before + piece_before
+        total = total.astype(F32) + sum(wide)
         stride *= radix
-        if stride < count:
-            total = total.astype(F32) + sum(came)
-    return before
+
+
+def merge_kernel(axis, stride, n, *refs):
+    outs = 2 * CHUNKS
+    ins, (send_refs, keep_refs) = refs[:-outs], (refs[-outs:][:CHUNKS], refs[-CHUNKS:])
+    bound_refs, came_refs = ins[:n], ins[n:]
+    extra = len(came_refs) & 1 ^ 1
+    base_ref, came_refs = (came_refs[0], came_refs[1:]) if extra else (None, came_refs)
+    digit = (lax.axis_index(axis) // stride) % (len(came_refs) + 1)
+    width = send_refs[0].shape[2]
+    for c in range(CHUNKS):
+        cols = pl.ds(c * width, width)
+        early = None if base_ref is None else base_ref[:, cols]
+        for k, came_ref in enumerate(came_refs, 1):
+            piece = jnp.where((digit ^ k) < digit, came_ref[:, cols].astype(F32), 0.0)
+            early = piece if early is None else early + piece
+        for k in range(n):
+            held = early + bound_refs[k][:, cols]
+            if k & 1:
+                send_refs[c][k // 2] = held.astype(BF16)
+            else:
+                keep_refs[c][k // 2] = held
+
+
+def near(value):
+    return pltpu.with_memory_space_constraint(value, pltpu.VMEM)
+
+
+def far(value):
+    return pltpu.with_memory_space_constraint(value, pltpu.HBM)
+
+
+def merged(held, got, bit):
+    kept = [k for k in held if not k & bit]
+    return {k: held[k] + got[i].astype(F32) for i, k in enumerate(kept)}
 
 
 def cost(flops, size):
@@ -208,7 +218,6 @@
     rows, depth = loaded.shape
     head = depth // H
     width = min(LANES, depth)
-    steps = depth // width
     cap = 2 * rows // n
     square = depth * depth
     table = jnp.swapaxes(packing, 2, 3)
@@ -219,27 +228,26 @@
     weight = pltpu.VMEM((depth, depth), BF16)
     params = pltpu.CompilerParams(vmem_limit_bytes=VMEM)
 
-    state, key, value = pl.pallas_call(
-        functools.partial(state_kernel, head, width),
-        in_specs=[hbm] * 3,
-        out_specs=[vmem] * 3,
-        out_shape=[shape((head, depth), BF16)] + [shape((rows, depth), BF16)] * 2,
-        scratch_shapes=[pltpu.VMEM((rows, depth), BF16), weight, weight]
-        + [pltpu.SemaphoreType.DMA((1 + 2 * steps,))],
-        cost_estimate=cost(4 * rows * square, 4 * square),
-        name="states",
-    )(loaded, w_key, w_value)
-    before = earlier_groups(state, "seqo")
     slots = pl.pallas_call(
         functools.partial(slot_kernel, "seqi"),
         in_specs=[smem, vmem],
         out_specs=[vmem] * (n - 1),
-        out_shape=[shape((cap, depth), BF16)] * (n - 1),
-        compiler_params=params,
-        cost_estimate=cost(4 * rows * rows * depth, 4 * rows * depth),
+        out_shape=[pltpu.VMEM((cap, depth), BF16)] * (n - 1),
+        compiler_params=params,
+        cost_estimate=cost(SLOTS_COST, 4 * rows * depth),
         name="slots",
-    )(table, loaded)
+    )(far(table), far(loaded))
     came = [swap(slots[k - 1], "seqi", k) for k in range(1, n)]
+    state, key, value = pl.pallas_call(
+        functools.partial(state_kernel, head, width),
+        in_specs=[vmem] * 3,
+        out_specs=[vmem] * 3,
+        out_shape=[pltpu.VMEM((head, depth), BF16)] + [pltpu.VMEM((rows, depth), BF16)] * 2,
+        compiler_params=params,
+        cost_estimate=cost(4 * rows * square, 4 * square),
+        name="states",
+    )(loaded, w_key, w_value)
+    before, groups, stride = earlier_groups(state, "seqo")
     bound = pl.pallas_call(
         functools.partial(bound_kernel, "seqi", head, width),
         in_specs=[smem, vmem, vmem],
@@ -250,26 +258,39 @@
         name="bounds",
     )(table, key, value)
 
-    held = {k: bound[k] if before is None else before + bound[k] for k in range(n)}
-    bit = 1
+    chunk = depth // CHUNKS
+    earlier = ([] if before is None else [before]) + groups
+    merge = pl.pallas_call(
+        functools.partial(merge_kernel, "seqo", stride, n),
+        in_specs=[vmem] * (n + len(earlier)),
+        out_specs=[vmem] * (2 * CHUNKS),
+        out_shape=[pltpu.VMEM((n // 2, head, chunk), BF16)] * CHUNKS
+        + [pltpu.VMEM((n // 2, head, chunk), F32)] * CHUNKS,
+        compiler_params=params,
+        cost_estimate=cost(2 * n * head * depth, 8 * n * head * depth),
+        name="merge",
+    )(*bound, *(near(piece) for piece in earlier))
+    parts, gate = [], None
+    for c in range(CHUNKS):
+        got = swap(merge[c], "seqi", 1)
+        parts.append(({k: merge[CHUNKS + c][k // 2] for k in range(0, n, 2)}, got))
+    bit = 2
     while bit < n:
-        send = [k for k in held if k & bit]
-        if len(send) > 1:
-            got = swap(jnp.stack([held[k].astype(BF16) for k in send]), "seqi", bit)
-        else:
-            got = [swap(held[send[0]].astype(BF16), "seqi", bit)]
-        if 2 * bit < n:
-            held = {k ^ bit: held[k ^ bit] + got[i].astype(F32) for i, k in enumerate(send)}
-        else:
-            last = got[0]
+        for c, (held, got) in enumerate(parts):
+            if c > 0:
+                got, _ = lax.optimization_barrier((got, gate))
+            held = merged(held, got, bit // 2)
+            send = [held[k].astype(BF16) for k in held if k & bit]
+            gate = jnp.stack(send) if len(send) > 1 else send[0][None]
+            parts[c] = held, swap(gate, "seqi", bit)
         bit *= 2
+    kept, last = [held[0] for held, _ in parts], [got[0] for _, got in parts]
 
     query, local = pl.pallas_call(
         functools.partial(local_kernel, "seqi", head, width),
-        in_specs=[smem, vmem, vmem] + [hbm] * 3 + [vmem] * (n - 1),
+        in_specs=[smem] + [vmem] * (n + 4),
         out_specs=[vmem] * 2,
         out_shape=[shape((rows, depth), BF16), shape((rows, depth), F32)],
-        scratch_shapes=[weight] * 3 + [pltpu.SemaphoreType.DMA((3 * steps,))],
         compiler_params=params,
         cost_estimate=cost(6 * rows * square, 6 * square),
         name="local",
@@ -277,14 +298,13 @@
 
     return pl.pallas_call(
         functools.partial(out_kernel, head, width),
-        in_specs=[vmem] * 5 + [hbm],
+        in_specs=[vmem] * (4 + 2 * CHUNKS),
         out_specs=vmem,
         out_shape=shape((rows, depth), F32),
-        scratch_shapes=[weight, pltpu.SemaphoreType.DMA((steps,))],
         compiler_params=params,
         cost_estimate=cost(2 * rows * square, 2 * square),
         name="out",
-    )(query, local, held[0], last, norm_gain.reshape(1, depth), w_out)
+    )(query, local, *kept, *last, norm_gain.reshape(1, depth), w_out)
 
 
 def solution(mesh):

time: 45 us -> 42.9 us (0.953)
  Pallas kernels: 16.9 us -> 9.93 us
  starting transfers between devices: 13.8 us -> 17.3 us
  local copies, waits for them, and re-layouts: 1.94 us -> 4.18 us
  waiting for transfers between devices: 11.7 us -> 11.1 us
    ppermute x8 -> x10, starting transfers between devices: 13.8 us -> 17.3 us  [swap(): lax.ppermute(value, axis, [(i, i ^ bits) for i in range(lax.axis_size(axi...]
    pallas_call x1 -> x2, Pallas kernels: 5.08 us -> 1.63 us  [the longest x1 1.5 us: body(): pl.pallas_call(functools.partial(state_kernel, head, width), in_specs=[vm...]
    pallas_call x1, Pallas kernels: 6.63 us -> 3.25 us  [body(): pl.pallas_call(functools.partial(local_kernel, 'seqi', head, width), in_s...]
    unnamed x20 -> x24, local copies, waits for them, and re-layouts: 1.94 us -> 4.18 us
    pallas_call x1, Pallas kernels: 3.02 us -> 2.34 us  [body(): pl.pallas_call(functools.partial(out_kernel, head, width), in_specs=[vmem...]
    ppermute x8 -> x10, waiting for transfers between devices: 11.7 us -> 11.1 us  [swap(): lax.ppermute(value, axis, [(i, i ^ bits) for i in range(lax.axis_size(axi...]
    pallas_call x1, Pallas kernels: 0.87 us -> 1.37 us  [body(): pl.pallas_call(functools.partial(slot_kernel, 'seqi'), in_specs=[smem, vm...]
  transfers between devices with their start and end apart: 8 -> 10, of which waited for: 4 -> 3; matrix products, arithmetic and copies ran while one was open for 0% -> 0% of each run, Pallas kernels for 20% -> 14%
where the time goes in v1:
time: 42.9 us; the launch traced here: 42.7 us
  starting transfers between devices  17.3 us (40%)
  waiting for transfers between devices  11.1 us (26%)
  Pallas kernels  9.93 us (23%)
  local copies, waits for them, and re-layouts  4.18 us (10%)
    ppermute x10, starting transfers between devices, swap(): lax.ppermute(value, axis, [(i, i ^ bits) for i in range(lax.axis_size(axi...  17.3 us
    ppermute x10, waiting for transfers between devices, swap(): lax.ppermute(value, axis, [(i, i ^ bits) for i in range(lax.axis_size(axi...  11.1 us
    unnamed x24, local copies, waits for them, and re-layouts  4.18 us
    pallas_call x1, Pallas kernels, body(): pl.pallas_call(functools.partial(local_kernel, 'seqi', head, width), in_s...  3.25 us
    pallas_call x1, Pallas kernels, body(): pl.pallas_call(functools.partial(out_kernel, head, width), in_specs=[vmem...  2.34 us
    pallas_call x1, Pallas kernels, body(): pl.pallas_call(functools.partial(state_kernel, head, width), in_specs=[vm...  1.5 us
    pallas_call x1, Pallas kernels, body(): pl.pallas_call(functools.partial(slot_kernel, 'seqi'), in_specs=[smem, vm...  1.37 us
    pallas_call x1, Pallas kernels, body(): pl.pallas_call(functools.partial(bound_kernel, 'seqi', head, width), in_s...  1.34 us
  transfers between devices with their start and end apart: 10, of which 3 were waited for; matrix products, arithmetic and copies ran while one was open for 0% of the time, Pallas kernels for 14%

profile of v1, /device:TPU:0, one launch (start us, length us, event | category | flops | bytes accessed | tf_op | source)
XLA Modules:
  0.0 42.7 jit_solution(3412580929727704853)
XLA Ops:
  0.0 0.0 copy-start
  0.0 1.6 %copy-done = bf16[1024,1024]{1,0:T(8,128)(2,1)S(1)} copy-done((bf16[1024,1024]{1,0:T(8,128)(2,1)S(1)}, bf16[1024,1024]{1,0:T(8,128)(2,1)}, u32[]{:S(2)}) %copy-start) | copy-done | bytes 2097176
  1.6 0.0 copy-start.2
  1.6 1.6 %copy-done.2 = bf16[1024,1024]{1,0:T(8,128)(2,1)S(1)} copy-done((bf16[1024,1024]{1,0:T(8,128)(2,1)S(1)}, bf16[1024,1024]{1,0:T(8,128)(2,1)}, u32[]{:S(2)}) %copy-start.2) | copy-done | bytes 2097176
  3.2 0.0 copy-start.6
  3.2 0.9 %copy-done.6 = bf16[128,1024]{1,0:T(8,128)(2,1)S(1)} copy-done((bf16[128,1024]{1,0:T(8,128)(2,1)S(1)}, bf16[128,1024]{1,0:T(8,128)(2,1)}, u32[]{:S(2)}) %copy-start.6) | copy-done | bytes 262168
  4.1 0.0 copy-start.9
  4.1 1.5 %states.1 = (bf16[64,1024]{1,0:T(8,128)(2,1)S(1)}, bf16[128,1024]{1,0:T(8,128)(2,1)S(1)}, bf16[128,1024]{1,0:T(8,128)(2,1)S(1)}) custom-call(bf16[128,1024]{1,0:T(8,128)(2,1)S(1)} %copy-done.6, bf16[1024,1024]{1,0:T(8,128)(2,1)S(1)} %copy-done, bf16[1024,1024]{1,0:T(8,128)(2,1)S(1)} %copy-done.2), custom_call_target="tpu_custom_call" | custom-call | flops 536870912 | bytes 4194304 | tf_op jit(solution)/shard_map/states/pallas_call | solution.py:241
  5.6 3.0 %collective-permute-start.3 = (bf16[64,1024]{1,0:T(8,128)(2,1)S(1)}, bf16[64,1024]{1,0:T(8,128)(2,1)S(1)}, u32[]{:S(2)}, u32[]{:S(2)}) collective-permute-start(bf16[64,1024]{1,0:T(8,128)(2,1)S(1)} %get-tuple-element.33), channel_id=1, source_target_pairs={{0,4},{4,0},{8,12},{12,8},{1,5},{5,1},{9,13},{13,9},{2,6},{6,2},{1... | collective-permute-start | bytes 393224 | tf_op jit(solution)/shard_map/ppermute | solution.py:157
  8.7 1.5 %collective-permute-start.4 = (bf16[64,1024]{1,0:T(8,128)(2,1)S(1)}, bf16[64,1024]{1,0:T(8,128)(2,1)S(1)}, u32[]{:S(2)}, u32[]{:S(2)}) collective-permute-start(bf16[64,1024]{1,0:T(8,128)(2,1)S(1)} %get-tuple-element.33), channel_id=1, source_target_pairs={{0,8},{4,12},{8,0},{12,4},{1,9},{5,13},{9,1},{13,5},{2,10},{6,14},... | collective-permute-start | bytes 393224 | tf_op jit(solution)/shard_map/ppermute | solution.py:157
  10.2 0.0 collective-permute-start.5
  10.2 0.0 copy-done.9
  10.2 1.3 %bounds.1 = (f32[64,1024]{1,0:T(8,128)S(1)}, f32[64,1024]{1,0:T(8,128)S(1)}, f32[64,1024]{1,0:T(8,128)S(1)}, f32[64,1024]{1,0:T(8,128)S(1)}) custom-call(s32[1,4,2,4]{3,2,1,0:T(2,128)S(1)} %bitcast.11, bf16[128,1024]{1,0:T(8,128)(2,1)S(1)} %get-tuple-element.27.key_ref, bf16[128,1024]{1,0:T(8,128)(2,1)S(1)} %get-tuple-element.28.value_ref), custom_call_target="tpu_custom_call" | custom-call | flops 268435456 | bytes 524288 | tf_op jit(solution)/shard_map/bounds/pallas_call | solution.py:251
  11.6 1.0 %collective-permute-done.3.refs_4_ = bf16[64,1024]{1,0:T(8,128)(2,1)S(1)} collective-permute-done((bf16[64,1024]{1,0:T(8,128)(2,1)S(1)}, bf16[64,1024]{1,0:T(8,128)(2,1)S(1)}, u32[]{:S(2)}, u32[]{:S(2)}) %collective-permute-start.3) | collective-permute-done | bytes 131104 | tf_op jit(solution)/shard_map/ppermute | solution.py:157
  12.6 3.9 %collective-permute-done.4.refs_5_ = bf16[64,1024]{1,0:T(8,128)(2,1)S(1)} collective-permute-done((bf16[64,1024]{1,0:T(8,128)(2,1)S(1)}, bf16[64,1024]{1,0:T(8,128)(2,1)S(1)}, u32[]{:S(2)}, u32[]{:S(2)}) %collective-permute-start.4) | collective-permute-done | bytes 131104 | tf_op jit(solution)/shard_map/ppermute | solution.py:157
  16.4 0.0 collective-permute-done.5.refs_6_
  16.5 0.1 merge.1
  16.6 0.0 copy-start.7
  16.6 0.0 copy-start.8
  16.6 0.0 copy-start.10
  16.6 1.6 %collective-permute-start.6 = (bf16[2,64,512]{2,1,0:T(8,128)(2,1)S(1)}, bf16[2,64,512]{2,1,0:T(8,128)(2,1)S(1)}, u32[]{:S(2)}, u32[]{:S(2)}) collective-permute-start(bf16[2,64,512]{2,1,0:T(8,128)(2,1)S(1)} %get-tuple-element.35), channel_id=1, source_target_pairs={{0,1},{1,0},{2,3},{3,2},{4,5},{5,4},{6,7},{7,6},{8,9},{9,8},{10,11... | collective-permute-start | bytes 393224 | tf_op jit(solution)/shard_map/ppermute | solution.py:157
  18.3 0.0 copy-start.1
  18.3 1.4 %slots.1 = (bf16[64,1024]{1,0:T(8,128)(2,1)S(1)}, bf16[64,1024]{1,0:T(8,128)(2,1)S(1)}, bf16[64,1024]{1,0:T(8,128)(2,1)S(1)}) custom-call(s32[1,4,2,4]{3,2,1,0:T(2,128)} %bitcast.10, bf16[128,1024]{1,0:T(8,128)(2,1)} %x_ref.5), custom_call_target="tpu_custom_call" | custom-call | flops 99999997952 | bytes 524288 | tf_op jit(solution)/shard_map/slots/pallas_call | solution.py:231
  19.7 0.5 %collective-permute-start = (bf16[64,1024]{1,0:T(8,128)(2,1)S(1)}, bf16[64,1024]{1,0:T(8,128)(2,1)S(1)}, u32[]{:S(2)}, u32[]{:S(2)}) collective-permute-start(bf16[64,1024]{1,0:T(8,128)(2,1)S(1)} %get-tuple-element.22), channel_id=1, source_target_pairs={{0,1},{1,0},{2,3},{3,2},{4,5},{5,4},{6,7},{7,6},{8,9},{9,8},{10,11... | collective-permute-start | bytes 393224 | tf_op jit(solution)/shard_map/ppermute | solution.py:157
  20.2 2.6 %collective-permute-start.1 = (bf16[64,1024]{1,0:T(8,128)(2,1)S(1)}, bf16[64,1024]{1,0:T(8,128)(2,1)S(1)}, u32[]{:S(2)}, u32[]{:S(2)}) collective-permute-start(bf16[64,1024]{1,0:T(8,128)(2,1)S(1)} %get-tuple-element.23), channel_id=1, source_target_pairs={{0,2},{1,3},{2,0},{3,1},{4,6},{5,7},{6,4},{7,5},{8,10},{9,11},{10,... | collective-permute-start | bytes 393224 | tf_op jit(solution)/shard_map/ppermute | solution.py:157
  22.8 1.3 %collective-permute-start.2 = (bf16[64,1024]{1,0:T(8,128)(2,1)S(1)}, bf16[64,1024]{1,0:T(8,128)(2,1)S(1)}, u32[]{:S(2)}, u32[]{:S(2)}) collective-permute-start(bf16[64,1024]{1,0:T(8,128)(2,1)S(1)} %get-tuple-element.24), channel_id=1, source_target_pairs={{0,3},{1,2},{2,1},{3,0},{4,7},{5,6},{6,5},{7,4},{8,11},{9,10},{10,... | collective-permute-start | bytes 393224 | tf_op jit(solution)/shard_map/ppermute | solution.py:157
  24.1 0.2 collective-permute-start.7
  24.3 0.0 collective-permute-done.6
  24.4 2.9 %collective-permute-start.8 = (bf16[1,64,512]{2,1,0:T(8,128)(2,1)S(1)}, bf16[1,64,512]{2,1,0:T(8,128)(2,1)S(1)}, u32[]{:S(2)}, u32[]{:S(2)}) collective-permute-start(bf16[1,64,512]{2,1,0:T(8,128)(2,1)S(1)} %get-tuple-element.41), channel_id=1, source_target_pairs={{0,2},{1,3},{2,0},{3,1},{4,6},{5,7},{6,4},{7,5},{8,10},{9,11},{10,... | collective-permute-start | bytes 196616 | tf_op jit(solution)/shard_map/ppermute | solution.py:157
  27.2 6.2 %collective-permute-done.7 = bf16[2,64,512]{2,1,0:T(8,128)(2,1)S(1)} collective-permute-done((bf16[2,64,512]{2,1,0:T(8,128)(2,1)S(1)}, bf16[2,64,512]{2,1,0:T(8,128)(2,1)S(1)}, u32[]{:S(2)}, u32[]{:S(2)}) %collective-permute-start.7) | collective-permute-done | bytes 131104 | tf_op jit(solution)/shard_map/ppermute | solution.py:157
  33.5 0.0 copy-start.5
  33.5 0.0 copy-start.11
  33.5 3.5 %collective-permute-start.9 = (bf16[1,64,512]{2,1,0:T(8,128)(2,1)S(1)}, bf16[1,64,512]{2,1,0:T(8,128)(2,1)S(1)}, u32[]{:S(2)}, u32[]{:S(2)}) collective-permute-start(bf16[1,64,512]{2,1,0:T(8,128)(2,1)S(1)} %get-tuple-element.39), channel_id=1, source_target_pairs={{0,2},{1,3},{2,0},{3,1},{4,6},{5,7},{6,4},{7,5},{8,10},{9,11},{10,... | collective-permute-start | bytes 196616 | tf_op jit(solution)/shard_map/ppermute | solution.py:157
  37.0 0.0 collective-permute-done.rest_0_
  37.0 0.0 collective-permute-done.1.rest_1_
  37.0 0.0 collective-permute-done.2.rest_2_
  37.0 0.0 copy-done.7
  37.0 0.0 copy-done.8
  37.0 0.0 copy-done.10
  37.1 0.0 copy-done.1
  37.1 0.0 copy-done.3
  37.1 0.0 copy-done.4
  37.1 3.3 %local.1 = (bf16[128,1024]{1,0:T(8,128)(2,1)S(1)}, f32[128,1024]{1,0:T(8,128)S(1)}) custom-call(s32[1,4,2,4]{3,2,1,0:T(2,128)S(1)} %bitcast.12, s32[1,64,64]{2,1,0:T(8,128)S(1)} %copy-done.8, bf16[128,1024]{1,0:T(8,128)(2,1)S(1)} %copy-done.7, bf16[1024,1024]{1,0:T(8,128)(2,1)S(1)} %copy-done.4, bf16[1024,1024]{1,0:T(8,128)(2,1)S(1)} %copy-done.1, ...), custom_call_target="tpu_custom_call" | custom-call | flops 805306368 | bytes 6291456 | tf_op jit(solution)/shard_map/local/pallas_call | solution.py:289
  40.3 0.0 collective-permute-done.9
  40.4 0.0 collective-permute-done.8
  40.4 0.0 copy-done.5
  40.4 0.0 copy-done.11
  40.4 2.3 %out.1 = f32[128,1024]{1,0:T(8,128)} custom-call(bf16[128,1024]{1,0:T(8,128)(2,1)S(1)} %get-tuple-element.25.q_ref, f32[128,1024]{1,0:T(8,128)S(1)} %get-tuple-element.26.local_ref, f32[64,512]{1,0:T(8,128)S(1)} %get-tuple-element.42.rest_0_, f32[64,512]{1,0:T(8,128)S(1)} %get-tuple-element.40.rest_1_, bf16[64,512]{1,0:T(8,128)(2,1)S(1)} %bitcast.8, ...), custom_call_target="tpu_custom_call" | custom-call | flops 268435456 | bytes 2097152 | tf_op jit(solution)/shard_map/out/pallas_call | solution.py:299
  (4 shorter events, 0.1 us)
Async XLA Ops:
  0.0 1.6 %copy-start = (bf16[1024,1024]{1,0:T(8,128)(2,1)S(1)}, bf16[1024,1024]{1,0:T(8,128)(2,1)}, u32[]{:S(2)}) copy-start(bf16[1024,1024]{1,0:T(8,128)(2,1)} %wk.3) | copy-start | bytes 6291460
  1.6 1.6 %copy-start.2 = (bf16[1024,1024]{1,0:T(8,128)(2,1)S(1)}, bf16[1024,1024]{1,0:T(8,128)(2,1)}, u32[]{:S(2)}) copy-start(bf16[1024,1024]{1,0:T(8,128)(2,1)} %wv.3) | copy-start | bytes 6291460
  3.2 0.9 %copy-start.6 = (bf16[128,1024]{1,0:T(8,128)(2,1)S(1)}, bf16[128,1024]{1,0:T(8,128)(2,1)}, u32[]{:S(2)}) copy-start(bf16[128,1024]{1,0:T(8,128)(2,1)} %x_ref.5) | copy-start | bytes 786436
  4.1 6.1 %copy-start.9 = (s32[1,4,4,2]{2,3,1,0:T(2,128)S(1)}, s32[1,4,4,2]{2,3,1,0:T(2,128)}, u32[]{:S(2)}) copy-start(s32[1,4,4,2]{2,3,1,0:T(2,128)} %param.9) | copy-start | bytes 388
  5.6 6.9 %collective-permute-start.3 = (bf16[64,1024]{1,0:T(8,128)(2,1)S(1)}, bf16[64,1024]{1,0:T(8,128)(2,1)S(1)}, u32[]{:S(2)}, u32[]{:S(2)}) collective-permute-start(bf16[64,1024]{1,0:T(8,128)(2,1)S(1)} %get-tuple-element.33), channel_id=1, source_target_pairs={{0,4},{4,0},{8,12},{12,8},{1,5},{5,1},{9,13},{13,9},{2,6},{6,2},{1... | collective-permute-start | bytes 393224 | tf_op jit(solution)/shard_map/ppermute | solution.py:157
  8.7 7.8 %collective-permute-start.4 = (bf16[64,1024]{1,0:T(8,128)(2,1)S(1)}, bf16[64,1024]{1,0:T(8,128)(2,1)S(1)}, u32[]{:S(2)}, u32[]{:S(2)}) collective-permute-start(bf16[64,1024]{1,0:T(8,128)(2,1)S(1)} %get-tuple-element.33), channel_id=1, source_target_pairs={{0,8},{4,12},{8,0},{12,4},{1,9},{5,13},{9,1},{13,5},{2,10},{6,14},... | collective-permute-start | bytes 393224 | tf_op jit(solution)/shard_map/ppermute | solution.py:157
  10.2 6.3 %collective-permute-start.5 = (bf16[64,1024]{1,0:T(8,128)(2,1)S(1)}, bf16[64,1024]{1,0:T(8,128)(2,1)S(1)}, u32[]{:S(2)}, u32[]{:S(2)}) collective-permute-start(bf16[64,1024]{1,0:T(8,128)(2,1)S(1)} %get-tuple-element.33), channel_id=1, source_target_pairs={{0,12},{4,8},{8,4},{12,0},{1,13},{5,9},{9,5},{13,1},{2,14},{6,10},... | collective-permute-start | bytes 393224 | tf_op jit(solution)/shard_map/ppermute | solution.py:157
  16.6 20.4 %copy-start.7 = (bf16[128,1024]{1,0:T(8,128)(2,1)S(1)}, bf16[128,1024]{1,0:T(8,128)(2,1)}, u32[]{:S(2)}) copy-start(bf16[128,1024]{1,0:T(8,128)(2,1)} %x_ref.5) | copy-start | bytes 786436
  16.6 20.4 %copy-start.8 = (s32[1,64,64]{2,1,0:T(8,128)S(1)}, s32[1,64,64]{2,1,0:T(8,128)}, u32[]{:S(2)}) copy-start(s32[1,64,64]{2,1,0:T(8,128)} %pattern_ref.1) | copy-start | bytes 49156
  16.6 20.4 %copy-start.10 = (s32[1,4,4,2]{2,3,1,0:T(2,128)S(1)}, s32[1,4,4,2]{2,3,1,0:T(2,128)}, u32[]{:S(2)}) copy-start(s32[1,4,4,2]{2,3,1,0:T(2,128)} %param.9) | copy-start | bytes 388
  16.6 7.7 %collective-permute-start.6 = (bf16[2,64,512]{2,1,0:T(8,128)(2,1)S(1)}, bf16[2,64,512]{2,1,0:T(8,128)(2,1)S(1)}, u32[]{:S(2)}, u32[]{:S(2)}) collective-permute-start(bf16[2,64,512]{2,1,0:T(8,128)(2,1)S(1)} %get-tuple-element.35), channel_id=1, source_target_pairs={{0,1},{1,0},{2,3},{3,2},{4,5},{5,4},{6,7},{7,6},{8,9},{9,8},{10,11... | collective-permute-start | bytes 393224 | tf_op jit(solution)/shard_map/ppermute | solution.py:157
  18.3 18.8 %copy-start.1 = (bf16[1024,1024]{1,0:T(8,128)(2,1)S(1)}, bf16[1024,1024]{1,0:T(8,128)(2,1)}, u32[]{:S(2)}) copy-start(bf16[1024,1024]{1,0:T(8,128)(2,1)} %wk.3) | copy-start | bytes 6291460
  18.3 18.8 %copy-start.3 = (bf16[1024,1024]{1,0:T(8,128)(2,1)S(1)}, bf16[1024,1024]{1,0:T(8,128)(2,1)}, u32[]{:S(2)}) copy-start(bf16[1024,1024]{1,0:T(8,128)(2,1)} %wv.3) | copy-start | bytes 6291460
  18.3 18.8 %copy-start.4 = (bf16[1024,1024]{1,0:T(8,128)(2,1)S(1)}, bf16[1024,1024]{1,0:T(8,128)(2,1)}, u32[]{:S(2)}) copy-start(bf16[1024,1024]{1,0:T(8,128)(2,1)} %wq.1) | copy-start | bytes 6291460
  19.7 17.4 %collective-permute-start = (bf16[64,1024]{1,0:T(8,128)(2,1)S(1)}, bf16[64,1024]{1,0:T(8,128)(2,1)S(1)}, u32[]{:S(2)}, u32[]{:S(2)}) collective-permute-start(bf16[64,1024]{1,0:T(8,128)(2,1)S(1)} %get-tuple-element.22), channel_id=1, source_target_pairs={{0,1},{1,0},{2,3},{3,2},{4,5},{5,4},{6,7},{7,6},{8,9},{9,8},{10,11... | collective-permute-start | bytes 393224 | tf_op jit(solution)/shard_map/ppermute | solution.py:157
  20.2 16.8 %collective-permute-start.1 = (bf16[64,1024]{1,0:T(8,128)(2,1)S(1)}, bf16[64,1024]{1,0:T(8,128)(2,1)S(1)}, u32[]{:S(2)}, u32[]{:S(2)}) collective-permute-start(bf16[64,1024]{1,0:T(8,128)(2,1)S(1)} %get-tuple-element.23), channel_id=1, source_target_pairs={{0,2},{1,3},{2,0},{3,1},{4,6},{5,7},{6,4},{7,5},{8,10},{9,11},{10,... | collective-permute-start | bytes 393224 | tf_op jit(solution)/shard_map/ppermute | solution.py:157
  22.8 14.3 %collective-permute-start.2 = (bf16[64,1024]{1,0:T(8,128)(2,1)S(1)}, bf16[64,1024]{1,0:T(8,128)(2,1)S(1)}, u32[]{:S(2)}, u32[]{:S(2)}) collective-permute-start(bf16[64,1024]{1,0:T(8,128)(2,1)S(1)} %get-tuple-element.24), channel_id=1, source_target_pairs={{0,3},{1,2},{2,1},{3,0},{4,7},{5,6},{6,5},{7,4},{8,11},{9,10},{10,... | collective-permute-start | bytes 393224 | tf_op jit(solution)/shard_map/ppermute | solution.py:157
  24.1 9.3 %collective-permute-start.7 = (bf16[2,64,512]{2,1,0:T(8,128)(2,1)S(1)}, bf16[2,64,512]{2,1,0:T(8,128)(2,1)S(1)}, u32[]{:S(2)}, u32[]{:S(2)}) collective-permute-start(bf16[2,64,512]{2,1,0:T(8,128)(2,1)S(1)} %get-tuple-element.37), channel_id=1, source_target_pairs={{0,1},{1,0},{2,3},{3,2},{4,5},{5,4},{6,7},{7,6},{8,9},{9,8},{10,11... | collective-permute-start | bytes 393224 | tf_op jit(solution)/shard_map/ppermute | solution.py:157
  24.4 16.0 %collective-permute-start.8 = (bf16[1,64,512]{2,1,0:T(8,128)(2,1)S(1)}, bf16[1,64,512]{2,1,0:T(8,128)(2,1)S(1)}, u32[]{:S(2)}, u32[]{:S(2)}) collective-permute-start(bf16[1,64,512]{2,1,0:T(8,128)(2,1)S(1)} %get-tuple-element.41), channel_id=1, source_target_pairs={{0,2},{1,3},{2,0},{3,1},{4,6},{5,7},{6,4},{7,5},{8,10},{9,11},{10,... | collective-permute-start | bytes 196616 | tf_op jit(solution)/shard_map/ppermute | solution.py:157
  33.5 6.9 %copy-start.5 = (bf16[1024,1024]{1,0:T(8,128)(2,1)S(1)}, bf16[1024,1024]{1,0:T(8,128)(2,1)}, u32[]{:S(2)}) copy-start(bf16[1024,1024]{1,0:T(8,128)(2,1)} %rest_5_.1) | copy-start | bytes 6291460
  33.5 6.9 %copy-start.11 = (f32[1024]{0:T(1024)S(1)}, f32[1024]{0:T(1024)}, u32[]{:S(2)}) copy-start(f32[1024]{0:T(1024)} %param.14) | copy-start | bytes 12292
  33.5 6.8 %collective-permute-start.9 = (bf16[1,64,512]{2,1,0:T(8,128)(2,1)S(1)}, bf16[1,64,512]{2,1,0:T(8,128)(2,1)S(1)}, u32[]{:S(2)}, u32[]{:S(2)}) collective-permute-start(bf16[1,64,512]{2,1,0:T(8,128)(2,1)S(1)} %get-tuple-element.39), channel_id=1, source_target_pairs={{0,2},{1,3},{2,0},{3,1},{4,6},{5,7},{6,4},{7,5},{8,10},{9,11},{10,... | collective-permute-start | bytes 196616 | tf_op jit(solution)/shard_map/ppermute | solution.py:157

commit v2 on v1

--- a/solution.py
+++ b/solution.py
@@ -47,7 +47,7 @@
     return out
 
 
-def state_kernel(head, width, x_ref, wk, wv, s_ref, key_ref, value_ref):
+def state_kernel(head, width, x_ref, wk, wv, key_ref, value_ref, s_ref):
     rows = x_ref[...]
     for j in range(rows.shape[1] // width):
         cols = pl.ds(j * width, width)
@@ -80,26 +80,34 @@
             m_ref[:, cols] = diagonal(mm_tn(key, kept), head)
 
 
-def local_kernel(axis, head, width, table, pattern_ref, x_ref, wq, wk, wv, *rest):
-    slots, (q_ref, local_ref) = rest[:-2], rest[-2:]
-    rows, depth = x_ref.shape
-    n, steps = len(slots) + 1, depth // width
-    me = lax.axis_index(axis)
+def unpack(axis, table, x_ref, slots):
+    rows, me = x_ref.shape[0], lax.axis_index(axis)
     total = None
-    for k in range(n):
+    for k, held_ref in enumerate((x_ref, *slots)):
         source = me ^ k
         start = jnp.int32(0)
-        for s in range(n):
+        for s in range(len(slots) + 1):
             start += jnp.where(s < source, table[0, s, 1, me], 0)
         count = table[0, source, 1, me]
-        held = x_ref[...] if k == 0 else slots[k - 1][...]
+        held = held_ref[...]
         first = table[0, me, 0, me] if k == 0 else 0
         row, slot = iota((rows, held.shape[0]), 0), iota((rows, held.shape[0]), 1)
         place = row - start
         pick = (slot == place + first) & (place >= 0) & (place < count)
         part = mm(pick.astype(BF16), held)
         total = part if total is None else total + part
-    x = total.astype(BF16)
+    return total.astype(BF16)
+
+
+def local_kernel(axis, head, width, place, *refs):
+    if place == 0:
+        (table, pattern_ref, x_ref, wq, wk, wv, *slots), (q_ref, local_ref, tokens_ref) = refs[:-3], refs[-3:]
+        x = unpack(axis, table, x_ref, slots)
+        tokens_ref[...] = x
+    else:
+        pattern_ref, tokens_ref, wq, wk, wv, q_ref, local_ref = refs
+        x = tokens_ref[...]
+    rows = x.shape[0]
     frames = pattern_ref.shape[1]
     per = rows // frames
     grow = (iota((rows, frames), 0) // per == iota((rows, frames), 1)).astype(BF16)
@@ -107,8 +115,8 @@
     allowed = mm_nt(mm(grow, seen).astype(BF16), grow) > 0.5
     heads = width // head
     column = iota((rows, width), 1) // head
-    for j in range(steps):
-        cols = pl.ds(j * width, width)
+    for j in range(q_ref.shape[1] // width):
+        inner, cols = pl.ds(j * width, width), pl.ds(place + j * width, width)
         query = mm(x, wq[:, cols]).astype(BF16)
         key = mm(x, wk[:, cols]).astype(BF16)
         value = mm(x, wv[:, cols]).astype(BF16)
@@ -118,28 +126,25 @@
         masked = jnp.concatenate(
             [jnp.where(allowed, scores[i * rows : (i + 1) * rows], 0.0) for i in range(heads)], axis=0
         ).astype(BF16)
-        local_ref[:, cols] = diagonal(mm(masked, value), head)
-        q_ref[:, cols] = query
-
-
-def out_kernel(head, width, q_ref, local_ref, *rest):
-    kept_refs, recv_refs, (gain_ref, w, out_ref) = rest[:CHUNKS], rest[CHUNKS:-3], rest[-3:]
-    _, depth = q_ref.shape
-    steps = depth // width
+        local_ref[:, inner] = diagonal(mm(masked, value), head)
+        q_ref[:, inner] = query
+
+
+def out_kernel(head, width, place, depth, q_ref, local_ref, kept_ref, recv_ref, gain_ref, w, *rest):
+    chunk = kept_ref.shape[1]
+    so_far, rest = (rest[0], rest[1:]) if place > 0 else (None, rest)
     heads = width // head
     same = iota((width, width), 0) // head == iota((width, width), 1) // head
     ones = same.astype(BF16)
     zero = jnp.zeros((width, width), BF16)
-    total = None
-    for j in range(steps):
-        cols = pl.ds(j * width, width)
-        chunk, place = divmod(j * width, depth // CHUNKS)
-        inner = pl.ds(place, width)
-        prefix = kept_refs[chunk][:, inner] + recv_refs[chunk][:, inner].astype(F32)
+    normed = []
+    for j in range(chunk // width):
+        inner, cols = pl.ds(j * width, width), pl.ds(place + j * width, width)
+        prefix = kept_ref[:, inner] + recv_ref[:, inner].astype(F32)
         high = prefix.astype(BF16)
         low = (prefix - high.astype(F32)).astype(BF16)
-        query = q_ref[:, cols]
-        attended = local_ref[:, cols]
+        query = q_ref[:, inner]
+        attended = local_ref[:, inner]
         for part in (high, low):
             spread = jnp.where(same, jnp.concatenate([part] * heads, axis=0), zero)
             attended = attended + mm(query, spread)
@@ -147,10 +152,22 @@
         sq_high = square.astype(BF16)
         sq_low = (square - sq_high.astype(F32)).astype(BF16)
         mean = (mm(sq_high, ones) + mm(sq_low, ones)) * (1.0 / head)
-        normed = (attended * lax.rsqrt(mean + EPSILON) * gain_ref[:, cols]).astype(BF16)
-        piece = mm(normed, w[pl.ds(j * width, width), :])
-        total = piece if total is None else total + piece
-    out_ref[...] = total
+        normed.append((attended * lax.rsqrt(mean + EPSILON) * gain_ref[:, cols]).astype(BF16))
+    normed = jnp.concatenate(normed, axis=1)
+    copies = []
+    for j in range(depth // width):
+        cols = pl.ds(j * width, width)
+        piece = mm(normed, w[pl.ds(place, chunk), cols])
+        piece = piece if so_far is None else so_far[:, cols] + piece
+        if place + chunk < depth:
+            rest[0][:, cols] = piece
+        else:
+            out_hbm, total, sems = rest
+            total[:, cols] = piece
+            copies.append(pltpu.make_async_copy(total.at[:, cols], out_hbm.at[:, cols], sems.at[j]))
+            copies[j].start()
+    for copy in copies:
+        copy.wait()
 
 
 def swap(value, axis, bits):
@@ -174,26 +191,23 @@
         stride *= radix
 
 
-def merge_kernel(axis, stride, n, *refs):
-    outs = 2 * CHUNKS
-    ins, (send_refs, keep_refs) = refs[:-outs], (refs[-outs:][:CHUNKS], refs[-CHUNKS:])
+def merge_kernel(axis, stride, place, *refs):
+    ins, (send_ref, keep_ref) = refs[:-2], refs[-2:]
+    n, width = 2 * send_ref.shape[0], send_ref.shape[2]
     bound_refs, came_refs = ins[:n], ins[n:]
-    extra = len(came_refs) & 1 ^ 1
-    base_ref, came_refs = (came_refs[0], came_refs[1:]) if extra else (None, came_refs)
+    early = None
+    if len(came_refs) % 2 == 0:
+        early, came_refs = came_refs[0][:, pl.ds(place, width)], came_refs[1:]
     digit = (lax.axis_index(axis) // stride) % (len(came_refs) + 1)
-    width = send_refs[0].shape[2]
-    for c in range(CHUNKS):
-        cols = pl.ds(c * width, width)
-        early = None if base_ref is None else base_ref[:, cols]
-        for k, came_ref in enumerate(came_refs, 1):
-            piece = jnp.where((digit ^ k) < digit, came_ref[:, cols].astype(F32), 0.0)
-            early = piece if early is None else early + piece
-        for k in range(n):
-            held = early + bound_refs[k][:, cols]
-            if k & 1:
-                send_refs[c][k // 2] = held.astype(BF16)
-            else:
-                keep_refs[c][k // 2] = held
+    for k, came_ref in enumerate(came_refs, 1):
+        piece = jnp.where((digit ^ k) < digit, came_ref[:, pl.ds(place, width)].astype(F32), 0.0)
+        early = piece if early is None else early + piece
+    for k in range(n):
+        held = early + bound_refs[k][:, pl.ds(place, width)]
+        if k & 1:
+            send_ref[k // 2] = held.astype(BF16)
+        else:
+            keep_ref[k // 2] = held
 
 
 def near(value):
@@ -218,7 +232,9 @@
     rows, depth = loaded.shape
     head = depth // H
     width = min(LANES, depth)
+    steps = depth // width
     cap = 2 * rows // n
+    chunk = depth // CHUNKS
     square = depth * depth
     table = jnp.swapaxes(packing, 2, 3)
     smem = pl.BlockSpec(memory_space=pltpu.SMEM)
@@ -237,17 +253,20 @@
         cost_estimate=cost(SLOTS_COST, 4 * rows * depth),
         name="slots",
     )(far(table), far(loaded))
-    came = [swap(slots[k - 1], "seqi", k) for k in range(1, n)]
-    state, key, value = pl.pallas_call(
+    came = []
+    for k in range(1, n):
+        came.append(swap(slots[k - 1], "seqi", k))
+    key, value, state = pl.pallas_call(
         functools.partial(state_kernel, head, width),
         in_specs=[vmem] * 3,
         out_specs=[vmem] * 3,
-        out_shape=[pltpu.VMEM((head, depth), BF16)] + [pltpu.VMEM((rows, depth), BF16)] * 2,
+        out_shape=[pltpu.VMEM((rows, depth), BF16)] * 2 + [pltpu.VMEM((head, depth), BF16)],
         compiler_params=params,
         cost_estimate=cost(4 * rows * square, 4 * square),
         name="states",
     )(loaded, w_key, w_value)
     before, groups, stride = earlier_groups(state, "seqo")
+    groups = groups if before is None else [before] + groups
     bound = pl.pallas_call(
         functools.partial(bound_kernel, "seqi", head, width),
         in_specs=[smem, vmem, vmem],
@@ -258,22 +277,22 @@
         name="bounds",
     )(table, key, value)
 
-    chunk = depth // CHUNKS
-    earlier = ([] if before is None else [before]) + groups
-    merge = pl.pallas_call(
-        functools.partial(merge_kernel, "seqo", stride, n),
-        in_specs=[vmem] * (n + len(earlier)),
-        out_specs=[vmem] * (2 * CHUNKS),
-        out_shape=[pltpu.VMEM((n // 2, head, chunk), BF16)] * CHUNKS
-        + [pltpu.VMEM((n // 2, head, chunk), F32)] * CHUNKS,
-        compiler_params=params,
-        cost_estimate=cost(2 * n * head * depth, 8 * n * head * depth),
-        name="merge",
-    )(*bound, *(near(piece) for piece in earlier))
     parts, gate = [], None
     for c in range(CHUNKS):
-        got = swap(merge[c], "seqi", 1)
-        parts.append(({k: merge[CHUNKS + c][k // 2] for k in range(0, n, 2)}, got))
+        send, keep = pl.pallas_call(
+            functools.partial(merge_kernel, "seqo", stride, c * chunk),
+            in_specs=[vmem] * (n + len(groups)),
+            out_specs=[vmem] * 2,
+            out_shape=[
+                pltpu.VMEM((n // 2, head, chunk), BF16),
+                pltpu.VMEM((n // 2, head, chunk), F32),
+            ],
+            compiler_params=params,
+            cost_estimate=cost(2 * n * head * chunk, 8 * n * head * chunk),
+            name="merge",
+        )(*bound, *(near(piece) for piece in groups))
+        got = swap(send, "seqi", 1)
+        parts.append(({k: keep[k // 2] for k in range(0, n, 2)}, got))
     bit = 2
     while bit < n:
         for c, (held, got) in enumerate(parts):
@@ -286,25 +305,43 @@
         bit *= 2
     kept, last = [held[0] for held, _ in parts], [got[0] for _, got in parts]
 
-    query, local = pl.pallas_call(
-        functools.partial(local_kernel, "seqi", head, width),
-        in_specs=[smem] + [vmem] * (n + 4),
-        out_specs=[vmem] * 2,
-        out_shape=[shape((rows, depth), BF16), shape((rows, depth), F32)],
-        compiler_params=params,
-        cost_estimate=cost(6 * rows * square, 6 * square),
-        name="local",
-    )(table, pattern, loaded, w_query, w_key, w_value, *came)
-
-    return pl.pallas_call(
-        functools.partial(out_kernel, head, width),
-        in_specs=[vmem] * (4 + 2 * CHUNKS),
-        out_specs=vmem,
-        out_shape=shape((rows, depth), F32),
-        compiler_params=params,
-        cost_estimate=cost(2 * rows * square, 2 * square),
-        name="out",
-    )(query, local, *kept, *last, norm_gain.reshape(1, depth), w_out)
+    query, local, tokens = [], [], None
+    for c in range(CHUNKS):
+        if c == 0:
+            specs, values = [smem] + [vmem] * (n + 4), (table, pattern, loaded, w_query, w_key, w_value, *came)
+        else:
+            specs, values = [vmem] * 5, (pattern, tokens, w_query, w_key, w_value)
+        outs = [pltpu.VMEM((rows, chunk), BF16), pltpu.VMEM((rows, chunk), F32)]
+        outs += [pltpu.VMEM((rows, depth), BF16)] if c == 0 else []
+        q_part, local_part, *rest = pl.pallas_call(
+            functools.partial(local_kernel, "seqi", head, width, c * chunk),
+            in_specs=specs,
+            out_specs=[vmem] * len(outs),
+            out_shape=outs,
+            compiler_params=params,
+            cost_estimate=cost(6 * rows * depth * chunk, 6 * depth * chunk),
+            name="local",
+        )(*values)
+        query.append(q_part)
+        local.append(local_part)
+        tokens = rest[0] if rest else tokens
+
+    gain, total = norm_gain.reshape(1, depth), []
+    for c in range(CHUNKS):
+        end = c == CHUNKS - 1
+        total = [
+            pl.pallas_call(
+                functools.partial(out_kernel, head, width, c * chunk, depth),
+                in_specs=[vmem] * (6 + len(total)),
+                out_specs=hbm if end else vmem,
+                out_shape=shape((rows, depth), F32) if end else pltpu.VMEM((rows, depth), F32),
+                scratch_shapes=[pltpu.VMEM((rows, depth), F32), pltpu.SemaphoreType.DMA((steps,))] * end,
+                compiler_params=params,
+                cost_estimate=cost(2 * rows * depth * chunk, 2 * depth * chunk),
+                name="out",
+            )(query[c], local[c], kept[c], last[c], gain, w_out, *total)
+        ]
+    return total[0]
 
 
 def solution(mesh):

time: 42.9 us -> 43.1 us (level)
    pallas_call x3 -> x6, Pallas kernels: 5.72 us -> 5.77 us  [the longest x2 3.53 us: body(): pl.pallas_call(functools.partial(local_kernel, 'seqi', head, width, c * c...]
  transfers between devices with their start and end apart: 10 -> 10, of which waited for: 3 -> 3; matrix products, arithmetic and copies ran while one was open for 0% -> 0% of each run, Pallas kernels for 14% -> 16%
where the time goes in v2:
time: 43.1 us; the launch traced here: 42.9 us
  starting transfers between devices  17.4 us (40%)
  waiting for transfers between devices  10.9 us (25%)
  Pallas kernels  9.98 us (23%)
  local copies, waits for them, and re-layouts  4.42 us (10%)
    ppermute x10, starting transfers between devices, swap(): lax.ppermute(value, axis, [(i, i ^ bits) for i in range(lax.axis_size(axi...  17.4 us
    ppermute x10, waiting for transfers between devices, swap(): lax.ppermute(value, axis, [(i, i ^ bits) for i in range(lax.axis_size(axi...  10.9 us
    unnamed x24, local copies, waits for them, and re-layouts  4.42 us
    pallas_call x2, Pallas kernels, body(): pl.pallas_call(functools.partial(local_kernel, 'seqi', head, width, c * c...  3.53 us
    pallas_call x2, Pallas kernels, body(): pl.pallas_call(functools.partial(out_kernel, head, width, c * chunk, dept...  2.09 us
    pallas_call x1, Pallas kernels, body(): pl.pallas_call(functools.partial(state_kernel, head, width), in_specs=[vm...  1.5 us
    pallas_call x1, Pallas kernels, body(): pl.pallas_call(functools.partial(slot_kernel, 'seqi'), in_specs=[smem, vm...  1.37 us
    pallas_call x1, Pallas kernels, body(): pl.pallas_call(functools.partial(bound_kernel, 'seqi', head, width), in_s...  1.34 us
  transfers between devices with their start and end apart: 10, of which 3 were waited for; matrix products, arithmetic and copies ran while one was open for 0% of the time, Pallas kernels for 16%

profile of v2, /device:TPU:0, one launch (start us, length us, event | category | flops | bytes accessed | tf_op | source)
XLA Modules:
  0.0 42.9 jit_solution(9826327797831703933)
XLA Ops:
  0.0 0.0 copy-start
  0.0 1.6 %copy-done = bf16[1024,1024]{1,0:T(8,128)(2,1)S(1)} copy-done((bf16[1024,1024]{1,0:T(8,128)(2,1)S(1)}, bf16[1024,1024]{1,0:T(8,128)(2,1)}, u32[]{:S(2)}) %copy-start) | copy-done | bytes 2097176
  1.6 1.6 %copy-done.2 = bf16[1024,1024]{1,0:T(8,128)(2,1)S(1)} copy-done((bf16[1024,1024]{1,0:T(8,128)(2,1)S(1)}, bf16[1024,1024]{1,0:T(8,128)(2,1)}, u32[]{:S(2)}) %copy-start.2) | copy-done | bytes 2097176
  3.2 0.9 %copy-done.6 = bf16[128,1024]{1,0:T(8,128)(2,1)S(1)} copy-done((bf16[128,1024]{1,0:T(8,128)(2,1)S(1)}, bf16[128,1024]{1,0:T(8,128)(2,1)}, u32[]{:S(2)}) %copy-start.6) | copy-done | bytes 262168
  4.1 1.5 %states.1 = (bf16[128,1024]{1,0:T(8,128)(2,1)S(1)}, bf16[128,1024]{1,0:T(8,128)(2,1)S(1)}, bf16[64,1024]{1,0:T(8,128)(2,1)S(1)}) custom-call(bf16[128,1024]{1,0:T(8,128)(2,1)S(1)} %copy-done.6, bf16[1024,1024]{1,0:T(8,128)(2,1)S(1)} %copy-done, bf16[1024,1024]{1,0:T(8,128)(2,1)S(1)} %copy-done.2), custom_call_target="tpu_custom_call" | custom-call | flops 536870912 | bytes 4194304 | tf_op jit(solution)/shard_map/states/pallas_call | solution.py:259
  5.6 3.0 %collective-permute-start.3 = (bf16[64,1024]{1,0:T(8,128)(2,1)S(1)}, bf16[64,1024]{1,0:T(8,128)(2,1)S(1)}, u32[]{:S(2)}, u32[]{:S(2)}) collective-permute-start(bf16[64,1024]{1,0:T(8,128)(2,1)S(1)} %get-tuple-element.37), channel_id=1, source_target_pairs={{0,4},{4,0},{8,12},{12,8},{1,5},{5,1},{9,13},{13,9},{2,6},{6,2},{1... | collective-permute-start | bytes 393224 | tf_op jit(solution)/shard_map/ppermute | solution.py:174
  8.7 1.5 %collective-permute-start.4 = (bf16[64,1024]{1,0:T(8,128)(2,1)S(1)}, bf16[64,1024]{1,0:T(8,128)(2,1)S(1)}, u32[]{:S(2)}, u32[]{:S(2)}) collective-permute-start(bf16[64,1024]{1,0:T(8,128)(2,1)S(1)} %get-tuple-element.37), channel_id=1, source_target_pairs={{0,8},{4,12},{8,0},{12,4},{1,9},{5,13},{9,1},{13,5},{2,10},{6,14},... | collective-permute-start | bytes 393224 | tf_op jit(solution)/shard_map/ppermute | solution.py:174
  10.2 0.0 collective-permute-start.5
  10.2 0.0 copy-done.10
  10.2 1.3 %bounds.1 = (f32[64,1024]{1,0:T(8,128)S(1)}, f32[64,1024]{1,0:T(8,128)S(1)}, f32[64,1024]{1,0:T(8,128)S(1)}, f32[64,1024]{1,0:T(8,128)S(1)}) custom-call(s32[1,4,2,4]{3,2,1,0:T(2,128)S(1)} %bitcast.13, bf16[128,1024]{1,0:T(8,128)(2,1)S(1)} %get-tuple-element.31.key_ref, bf16[128,1024]{1,0:T(8,128)(2,1)S(1)} %get-tuple-element.32.value_ref), custom_call_target="tpu_custom_call" | custom-call | flops 268435456 | bytes 524288 | tf_op jit(solution)/shard_map/bounds/pallas_call | solution.py:270
  11.6 1.0 %collective-permute-done.3.refs_4_ = bf16[64,1024]{1,0:T(8,128)(2,1)S(1)} collective-permute-done((bf16[64,1024]{1,0:T(8,128)(2,1)S(1)}, bf16[64,1024]{1,0:T(8,128)(2,1)S(1)}, u32[]{:S(2)}, u32[]{:S(2)}) %collective-permute-start.3) | collective-permute-done | bytes 131104 | tf_op jit(solution)/shard_map/ppermute | solution.py:174
  12.6 3.9 %collective-permute-done.4.refs_5_ = bf16[64,1024]{1,0:T(8,128)(2,1)S(1)} collective-permute-done((bf16[64,1024]{1,0:T(8,128)(2,1)S(1)}, bf16[64,1024]{1,0:T(8,128)(2,1)S(1)}, u32[]{:S(2)}, u32[]{:S(2)}) %collective-permute-start.4) | collective-permute-done | bytes 131104 | tf_op jit(solution)/shard_map/ppermute | solution.py:174
  16.4 0.0 collective-permute-done.5.refs_6_
  16.5 0.1 merge.3
  16.5 1.6 %collective-permute-start.7 = (bf16[2,64,512]{2,1,0:T(8,128)(2,1)S(1)}, bf16[2,64,512]{2,1,0:T(8,128)(2,1)S(1)}, u32[]{:S(2)}, u32[]{:S(2)}) collective-permute-start(bf16[2,64,512]{2,1,0:T(8,128)(2,1)S(1)} %get-tuple-element.41), channel_id=1, source_target_pairs={{0,1},{1,0},{2,3},{3,2},{4,5},{5,4},{6,7},{7,6},{8,9},{9,8},{10,11... | collective-permute-start | bytes 393224 | tf_op jit(solution)/shard_map/ppermute | solution.py:174
  18.2 1.4 %slots.1 = (bf16[64,1024]{1,0:T(8,128)(2,1)S(1)}, bf16[64,1024]{1,0:T(8,128)(2,1)S(1)}, bf16[64,1024]{1,0:T(8,128)(2,1)S(1)}) custom-call(s32[1,4,2,4]{3,2,1,0:T(2,128)} %bitcast.12, bf16[128,1024]{1,0:T(8,128)(2,1)} %x_ref.3), custom_call_target="tpu_custom_call" | custom-call | flops 99999997952 | bytes 524288 | tf_op jit(solution)/shard_map/slots/pallas_call | solution.py:247
  19.6 0.0 copy-start.1
  19.6 0.0 copy-start.7
  19.6 0.0 copy-start.8
  19.6 0.0 copy-start.11
  19.6 0.5 %collective-permute-start = (bf16[64,1024]{1,0:T(8,128)(2,1)S(1)}, bf16[64,1024]{1,0:T(8,128)(2,1)S(1)}, u32[]{:S(2)}, u32[]{:S(2)}) collective-permute-start(bf16[64,1024]{1,0:T(8,128)(2,1)S(1)} %get-tuple-element.25), channel_id=1, source_target_pairs={{0,1},{1,0},{2,3},{3,2},{4,5},{5,4},{6,7},{7,6},{8,9},{9,8},{10,11... | collective-permute-start | bytes 393224 | tf_op jit(solution)/shard_map/ppermute | solution.py:174
  20.1 2.6 %collective-permute-start.1 = (bf16[64,1024]{1,0:T(8,128)(2,1)S(1)}, bf16[64,1024]{1,0:T(8,128)(2,1)S(1)}, u32[]{:S(2)}, u32[]{:S(2)}) collective-permute-start(bf16[64,1024]{1,0:T(8,128)(2,1)S(1)} %get-tuple-element.26), channel_id=1, source_target_pairs={{0,2},{1,3},{2,0},{3,1},{4,6},{5,7},{6,4},{7,5},{8,10},{9,11},{10,... | collective-permute-start | bytes 393224 | tf_op jit(solution)/shard_map/ppermute | solution.py:174
  22.7 1.4 %collective-permute-start.2 = (bf16[64,1024]{1,0:T(8,128)(2,1)S(1)}, bf16[64,1024]{1,0:T(8,128)(2,1)S(1)}, u32[]{:S(2)}, u32[]{:S(2)}) collective-permute-start(bf16[64,1024]{1,0:T(8,128)(2,1)S(1)} %get-tuple-element.27), channel_id=1, source_target_pairs={{0,3},{1,2},{2,1},{3,0},{4,7},{5,6},{6,5},{7,4},{8,11},{9,10},{10,... | collective-permute-start | bytes 393224 | tf_op jit(solution)/shard_map/ppermute | solution.py:174
  24.1 0.1 merge.2
  24.1 0.3 collective-permute-start.6
  24.4 0.0 collective-permute-done.7
  24.5 2.9 %collective-permute-start.9 = (bf16[1,64,512]{2,1,0:T(8,128)(2,1)S(1)}, bf16[1,64,512]{2,1,0:T(8,128)(2,1)S(1)}, u32[]{:S(2)}, u32[]{:S(2)}) collective-permute-start(bf16[1,64,512]{2,1,0:T(8,128)(2,1)S(1)} %get-tuple-element.46), channel_id=1, source_target_pairs={{0,2},{1,3},{2,0},{3,1},{4,6},{5,7},{6,4},{7,5},{8,10},{9,11},{10,... | collective-permute-start | bytes 196616 | tf_op jit(solution)/shard_map/ppermute | solution.py:174
  27.3 6.0 %collective-permute-done.6 = bf16[2,64,512]{2,1,0:T(8,128)(2,1)S(1)} collective-permute-done((bf16[2,64,512]{2,1,0:T(8,128)(2,1)S(1)}, bf16[2,64,512]{2,1,0:T(8,128)(2,1)S(1)}, u32[]{:S(2)}, u32[]{:S(2)}) %collective-permute-start.6) | collective-permute-done | bytes 131104 | tf_op jit(solution)/shard_map/ppermute | solution.py:174
  33.3 3.6 %collective-permute-start.8 = (bf16[1,64,512]{2,1,0:T(8,128)(2,1)S(1)}, bf16[1,64,512]{2,1,0:T(8,128)(2,1)S(1)}, u32[]{:S(2)}, u32[]{:S(2)}) collective-permute-start(bf16[1,64,512]{2,1,0:T(8,128)(2,1)S(1)} %get-tuple-element.47), channel_id=1, source_target_pairs={{0,2},{1,3},{2,0},{3,1},{4,6},{5,7},{6,4},{7,5},{8,10},{9,11},{10,... | collective-permute-start | bytes 196616 | tf_op jit(solution)/shard_map/ppermute | solution.py:174
  36.9 0.0 collective-permute-done.refs_6_
  36.9 0.0 collective-permute-done.1.refs_7_
  36.9 0.0 collective-permute-done.2.refs_8_
  36.9 0.0 copy-done.3
  36.9 0.0 copy-done.4
  36.9 0.0 copy-done.1
  36.9 0.0 copy-done.7
  37.0 0.0 copy-done.8
  37.0 0.0 copy-done.11
  37.0 2.2 %local.2 = (bf16[128,512]{1,0:T(8,128)(2,1)S(1)}, f32[128,512]{1,0:T(8,128)S(1)}, bf16[128,1024]{1,0:T(8,128)(2,1)S(1)}) custom-call(s32[1,4,2,4]{3,2,1,0:T(2,128)S(1)} %bitcast.14, s32[1,64,64]{2,1,0:T(8,128)S(1)} %copy-done.8, bf16[128,1024]{1,0:T(8,128)(2,1)S(1)} %copy-done.7, bf16[1024,1024]{1,0:T(8,128)(2,1)S(1)} %copy-done.4, ...), custom_call_target="tpu_custom_call" | custom-call | flops 402653184 | bytes 3145728 | tf_op jit(solution)/shard_map/local/pallas_call | solution.py:316
  39.2 0.0 copy-start.5
  39.2 0.0 copy-start.9
  39.2 1.3 %local.3 = (bf16[128,512]{1,0:T(8,128)(2,1)S(1)}, f32[128,512]{1,0:T(8,128)S(1)}) custom-call(s32[1,64,64]{2,1,0:T(8,128)S(1)} %copy-done.8, bf16[128,1024]{1,0:T(8,128)(2,1)S(1)} %get-tuple-element.28.refs_1_, bf16[1024,1024]{1,0:T(8,128)(2,1)S(1)} %copy-done.4, bf16[1024,1024]{1,0:T(8,128)(2,1)S(1)} %copy-done.1, bf16[1024,1024]{1,0:T(8,128)(2,1)S(1)} %copy-done.3), custom_call_target="tpu_custom_call" | custom-call | flops 402653184 | bytes 3145728 | tf_op jit(solution)/shard_map/local/pallas_call | solution.py:316
  40.5 0.0 collective-permute-done.9
  40.6 0.2 copy-done.5
  40.8 0.0 copy-done.9
  40.8 0.7 %out.2.rest_0_ = f32[128,1024]{1,0:T(8,128)S(1)} custom-call(bf16[128,512]{1,0:T(8,128)(2,1)S(1)} %get-tuple-element.43.q_ref, f32[128,512]{1,0:T(8,128)S(1)} %get-tuple-element.44.local_ref, f32[64,512]{1,0:T(8,128)S(1)} %get-tuple-element.45.kept_ref, bf16[64,512]{1,0:T(8,128)(2,1)S(1)} %bitcast.9, f32[1,1024]{1,0:T(1,128)S(1)} %bitcast.10, ...), custom_call_target="tpu_custom_call" | custom-call | flops 134217728 | bytes 1048576 | tf_op jit(solution)/shard_map/out/pallas_call | solution.py:333
  41.5 0.0 collective-permute-done.8
  41.5 1.4 %out.3 = f32[128,1024]{1,0:T(8,128)} custom-call(bf16[128,512]{1,0:T(8,128)(2,1)S(1)} %get-tuple-element.29.q_ref, f32[128,512]{1,0:T(8,128)S(1)} %get-tuple-element.30.local_ref, f32[64,512]{1,0:T(8,128)S(1)} %get-tuple-element.48.kept_ref, bf16[64,512]{1,0:T(8,128)(2,1)S(1)} %bitcast.8, f32[1,1024]{1,0:T(1,128)S(1)} %bitcast.11, ...), custom_call_target="tpu_custom_call" | custom-call | flops 134217728 | bytes 1048576 | tf_op jit(solution)/shard_map/out/pallas_call | solution.py:333
  (7 shorter events, 0.1 us)
Async XLA Ops:
  0.0 1.6 %copy-start = (bf16[1024,1024]{1,0:T(8,128)(2,1)S(1)}, bf16[1024,1024]{1,0:T(8,128)(2,1)}, u32[]{:S(2)}) copy-start(bf16[1024,1024]{1,0:T(8,128)(2,1)} %wk.1) | copy-start | bytes 6291460
  1.6 1.6 %copy-start.2 = (bf16[1024,1024]{1,0:T(8,128)(2,1)S(1)}, bf16[1024,1024]{1,0:T(8,128)(2,1)}, u32[]{:S(2)}) copy-start(bf16[1024,1024]{1,0:T(8,128)(2,1)} %wv.1) | copy-start | bytes 6291460
  3.2 0.9 %copy-start.6 = (bf16[128,1024]{1,0:T(8,128)(2,1)S(1)}, bf16[128,1024]{1,0:T(8,128)(2,1)}, u32[]{:S(2)}) copy-start(bf16[128,1024]{1,0:T(8,128)(2,1)} %x_ref.3) | copy-start | bytes 786436
  4.1 6.1 %copy-start.10 = (s32[1,4,4,2]{2,3,1,0:T(2,128)S(1)}, s32[1,4,4,2]{2,3,1,0:T(2,128)}, u32[]{:S(2)}) copy-start(s32[1,4,4,2]{2,3,1,0:T(2,128)} %param.9) | copy-start | bytes 388
  5.6 6.9 %collective-permute-start.3 = (bf16[64,1024]{1,0:T(8,128)(2,1)S(1)}, bf16[64,1024]{1,0:T(8,128)(2,1)S(1)}, u32[]{:S(2)}, u32[]{:S(2)}) collective-permute-start(bf16[64,1024]{1,0:T(8,128)(2,1)S(1)} %get-tuple-element.37), channel_id=1, source_target_pairs={{0,4},{4,0},{8,12},{12,8},{1,5},{5,1},{9,13},{13,9},{2,6},{6,2},{1... | collective-permute-start | bytes 393224 | tf_op jit(solution)/shard_map/ppermute | solution.py:174
  8.7 7.8 %collective-permute-start.4 = (bf16[64,1024]{1,0:T(8,128)(2,1)S(1)}, bf16[64,1024]{1,0:T(8,128)(2,1)S(1)}, u32[]{:S(2)}, u32[]{:S(2)}) collective-permute-start(bf16[64,1024]{1,0:T(8,128)(2,1)S(1)} %get-tuple-element.37), channel_id=1, source_target_pairs={{0,8},{4,12},{8,0},{12,4},{1,9},{5,13},{9,1},{13,5},{2,10},{6,14},... | collective-permute-start | bytes 393224 | tf_op jit(solution)/shard_map/ppermute | solution.py:174
  10.2 6.3 %collective-permute-start.5 = (bf16[64,1024]{1,0:T(8,128)(2,1)S(1)}, bf16[64,1024]{1,0:T(8,128)(2,1)S(1)}, u32[]{:S(2)}, u32[]{:S(2)}) collective-permute-start(bf16[64,1024]{1,0:T(8,128)(2,1)S(1)} %get-tuple-element.37), channel_id=1, source_target_pairs={{0,12},{4,8},{8,4},{12,0},{1,13},{5,9},{9,5},{13,1},{2,14},{6,10},... | collective-permute-start | bytes 393224 | tf_op jit(solution)/shard_map/ppermute | solution.py:174
  16.5 7.9 %collective-permute-start.7 = (bf16[2,64,512]{2,1,0:T(8,128)(2,1)S(1)}, bf16[2,64,512]{2,1,0:T(8,128)(2,1)S(1)}, u32[]{:S(2)}, u32[]{:S(2)}) collective-permute-start(bf16[2,64,512]{2,1,0:T(8,128)(2,1)S(1)} %get-tuple-element.41), channel_id=1, source_target_pairs={{0,1},{1,0},{2,3},{3,2},{4,5},{5,4},{6,7},{7,6},{8,9},{9,8},{10,11... | collective-permute-start | bytes 393224 | tf_op jit(solution)/shard_map/ppermute | solution.py:174
  18.2 18.7 %copy-start.3 = (bf16[1024,1024]{1,0:T(8,128)(2,1)S(1)}, bf16[1024,1024]{1,0:T(8,128)(2,1)}, u32[]{:S(2)}) copy-start(bf16[1024,1024]{1,0:T(8,128)(2,1)} %wv.1) | copy-start | bytes 6291460
  18.2 18.7 %copy-start.4 = (bf16[1024,1024]{1,0:T(8,128)(2,1)S(1)}, bf16[1024,1024]{1,0:T(8,128)(2,1)}, u32[]{:S(2)}) copy-start(bf16[1024,1024]{1,0:T(8,128)(2,1)} %refs_2_.3) | copy-start | bytes 6291460
  19.6 17.4 %copy-start.1 = (bf16[1024,1024]{1,0:T(8,128)(2,1)S(1)}, bf16[1024,1024]{1,0:T(8,128)(2,1)}, u32[]{:S(2)}) copy-start(bf16[1024,1024]{1,0:T(8,128)(2,1)} %wk.1) | copy-start | bytes 6291460
  19.6 17.4 %copy-start.7 = (bf16[128,1024]{1,0:T(8,128)(2,1)S(1)}, bf16[128,1024]{1,0:T(8,128)(2,1)}, u32[]{:S(2)}) copy-start(bf16[128,1024]{1,0:T(8,128)(2,1)} %x_ref.3) | copy-start | bytes 786436
  19.6 17.4 %copy-start.8 = (s32[1,64,64]{2,1,0:T(8,128)S(1)}, s32[1,64,64]{2,1,0:T(8,128)}, u32[]{:S(2)}) copy-start(s32[1,64,64]{2,1,0:T(8,128)} %refs_0_.1) | copy-start | bytes 49156
  19.6 17.4 %copy-start.11 = (s32[1,4,4,2]{2,3,1,0:T(2,128)S(1)}, s32[1,4,4,2]{2,3,1,0:T(2,128)}, u32[]{:S(2)}) copy-start(s32[1,4,4,2]{2,3,1,0:T(2,128)} %param.9) | copy-start | bytes 388
  19.6 17.3 %collective-permute-start = (bf16[64,1024]{1,0:T(8,128)(2,1)S(1)}, bf16[64,1024]{1,0:T(8,128)(2,1)S(1)}, u32[]{:S(2)}, u32[]{:S(2)}) collective-permute-start(bf16[64,1024]{1,0:T(8,128)(2,1)S(1)} %get-tuple-element.25), channel_id=1, source_target_pairs={{0,1},{1,0},{2,3},{3,2},{4,5},{5,4},{6,7},{7,6},{8,9},{9,8},{10,11... | collective-permute-start | bytes 393224 | tf_op jit(solution)/shard_map/ppermute | solution.py:174
  20.1 16.8 %collective-permute-start.1 = (bf16[64,1024]{1,0:T(8,128)(2,1)S(1)}, bf16[64,1024]{1,0:T(8,128)(2,1)S(1)}, u32[]{:S(2)}, u32[]{:S(2)}) collective-permute-start(bf16[64,1024]{1,0:T(8,128)(2,1)S(1)} %get-tuple-element.26), channel_id=1, source_target_pairs={{0,2},{1,3},{2,0},{3,1},{4,6},{5,7},{6,4},{7,5},{8,10},{9,11},{10,... | collective-permute-start | bytes 393224 | tf_op jit(solution)/shard_map/ppermute | solution.py:174
  22.7 14.2 %collective-permute-start.2 = (bf16[64,1024]{1,0:T(8,128)(2,1)S(1)}, bf16[64,1024]{1,0:T(8,128)(2,1)S(1)}, u32[]{:S(2)}, u32[]{:S(2)}) collective-permute-start(bf16[64,1024]{1,0:T(8,128)(2,1)S(1)} %get-tuple-element.27), channel_id=1, source_target_pairs={{0,3},{1,2},{2,1},{3,0},{4,7},{5,6},{6,5},{7,4},{8,11},{9,10},{10,... | collective-permute-start | bytes 393224 | tf_op jit(solution)/shard_map/ppermute | solution.py:174
  24.1 9.2 %collective-permute-start.6 = (bf16[2,64,512]{2,1,0:T(8,128)(2,1)S(1)}, bf16[2,64,512]{2,1,0:T(8,128)(2,1)S(1)}, u32[]{:S(2)}, u32[]{:S(2)}) collective-permute-start(bf16[2,64,512]{2,1,0:T(8,128)(2,1)S(1)} %get-tuple-element.39), channel_id=1, source_target_pairs={{0,1},{1,0},{2,3},{3,2},{4,5},{5,4},{6,7},{7,6},{8,9},{9,8},{10,11... | collective-permute-start | bytes 393224 | tf_op jit(solution)/shard_map/ppermute | solution.py:174
  24.5 16.1 %collective-permute-start.9 = (bf16[1,64,512]{2,1,0:T(8,128)(2,1)S(1)}, bf16[1,64,512]{2,1,0:T(8,128)(2,1)S(1)}, u32[]{:S(2)}, u32[]{:S(2)}) collective-permute-start(bf16[1,64,512]{2,1,0:T(8,128)(2,1)S(1)} %get-tuple-element.46), channel_id=1, source_target_pairs={{0,2},{1,3},{2,0},{3,1},{4,6},{5,7},{6,4},{7,5},{8,10},{9,11},{10,... | collective-permute-start | bytes 196616 | tf_op jit(solution)/shard_map/ppermute | solution.py:174
  33.3 8.1 %collective-permute-start.8 = (bf16[1,64,512]{2,1,0:T(8,128)(2,1)S(1)}, bf16[1,64,512]{2,1,0:T(8,128)(2,1)S(1)}, u32[]{:S(2)}, u32[]{:S(2)}) collective-permute-start(bf16[1,64,512]{2,1,0:T(8,128)(2,1)S(1)} %get-tuple-element.47), channel_id=1, source_target_pairs={{0,2},{1,3},{2,0},{3,1},{4,6},{5,7},{6,4},{7,5},{8,10},{9,11},{10,... | collective-permute-start | bytes 196616 | tf_op jit(solution)/shard_map/ppermute | solution.py:174
  39.2 1.6 %copy-start.5 = (bf16[1024,1024]{1,0:T(8,128)(2,1)S(1)}, bf16[1024,1024]{1,0:T(8,128)(2,1)}, u32[]{:S(2)}) copy-start(bf16[1024,1024]{1,0:T(8,128)(2,1)} %w.3) | copy-start | bytes 6291460
  39.2 1.6 %copy-start.9 = (f32[1024]{0:T(1024)S(1)}, f32[1024]{0:T(1024)}, u32[]{:S(2)}) copy-start(f32[1024]{0:T(1024)} %param.14) | copy-start | bytes 12292

commit v3 on v2

--- a/solution.py
+++ b/solution.py
@@ -60,12 +60,14 @@
 def slot_kernel(axis, table, x_ref, *slot_refs):
     me = lax.axis_index(axis)
     rows, cap = x_ref.shape[0], slot_refs[0].shape[0]
-    x = x_ref[...]
     slot, row = iota((cap, rows), 0), iota((cap, rows), 1)
-    for k, slot_ref in enumerate(slot_refs, 1):
+    picks = []
+    for k in range(1, len(slot_refs) + 1):
         first, count = table[0, me, 0, me ^ k], table[0, me, 1, me ^ k]
-        pick = jnp.logical_and(row == first + slot, slot < count)
-        slot_ref[...] = mm(pick.astype(BF16), x).astype(BF16)
+        picks.append(jnp.logical_and(row == first + slot, slot < count).astype(BF16))
+    picked = mm(jnp.concatenate(picks, axis=0), x_ref[...]).astype(BF16)
+    for k, slot_ref in enumerate(slot_refs):
+        slot_ref[...] = picked[k * cap : (k + 1) * cap]
 
 
 def bound_kernel(axis, head, width, table, key_ref, value_ref, *m_refs):
@@ -82,21 +84,21 @@
 
 def unpack(axis, table, x_ref, slots):
     rows, me = x_ref.shape[0], lax.axis_index(axis)
-    total = None
+    picks, held = [], []
     for k, held_ref in enumerate((x_ref, *slots)):
         source = me ^ k
         start = jnp.int32(0)
         for s in range(len(slots) + 1):
             start += jnp.where(s < source, table[0, s, 1, me], 0)
         count = table[0, source, 1, me]
-        held = held_ref[...]
         first = table[0, me, 0, me] if k == 0 else 0
-        row, slot = iota((rows, held.shape[0]), 0), iota((rows, held.shape[0]), 1)
+        shape = rows, held_ref.shape[0]
+        row, slot = iota(shape, 0), iota(shape, 1)
         place = row - start
         pick = (slot == place + first) & (place >= 0) & (place < count)
-        part = mm(pick.astype(BF16), held)
-        total = part if total is None else total + part
-    return total.astype(BF16)
+        picks.append(pick.astype(BF16))
+        held.append(held_ref[...])
+    return mm(jnp.concatenate(picks, axis=1), jnp.concatenate(held, axis=0)).astype(BF16)
 
 
 def local_kernel(axis, head, width, place, *refs):
@@ -130,8 +132,9 @@
         q_ref[:, inner] = query
 
 
-def out_kernel(head, width, place, depth, q_ref, local_ref, kept_ref, recv_ref, gain_ref, w, *rest):
-    chunk = kept_ref.shape[1]
+def out_kernel(head, width, place, depth, steps, q_ref, local_ref, gain_ref, w, final_ref, kept_ref, *rest):
+    chunk = final_ref.shape[1]
+    landed, rest = rest[:steps], rest[steps:]
     so_far, rest = (rest[0], rest[1:]) if place > 0 else (None, rest)
     heads = width // head
     same = iota((width, width), 0) // head == iota((width, width), 1) // head
@@ -140,7 +143,9 @@
     normed = []
     for j in range(chunk // width):
         inner, cols = pl.ds(j * width, width), pl.ds(place + j * width, width)
-        prefix = kept_ref[:, inner] + recv_ref[:, inner].astype(F32)
+        prefix = kept_ref[:, cols] + final_ref[:, inner].astype(F32)
+        for ref in landed:
+            prefix = prefix + ref[:, cols].astype(F32)
         high = prefix.astype(BF16)
         low = (prefix - high.astype(F32)).astype(BF16)
         query = q_ref[:, inner]
@@ -179,7 +184,9 @@
     before, total, stride = None, state, 1
     while True:
         radix = min(4, count // stride)
-        came = [swap(total.astype(BF16), axis, k * stride) for k in range(1, radix)]
+        came = []
+        for k in range(1, radix):
+            came.append(swap(total.astype(BF16), axis, k * stride))
         if stride * radix >= count:
             return before, came, stride
         digit = (mine // stride) % radix
@@ -191,23 +198,23 @@
         stride *= radix
 
 
-def merge_kernel(axis, stride, place, *refs):
-    ins, (send_ref, keep_ref) = refs[:-2], refs[-2:]
-    n, width = 2 * send_ref.shape[0], send_ref.shape[2]
-    bound_refs, came_refs = ins[:n], ins[n:]
+def merge_kernel(axis, stride, n, *refs):
+    bound_refs, came_refs, outs = refs[:n], list(refs[n : -(n // 2 + 2)]), refs[-(n // 2 + 2) :]
     early = None
     if len(came_refs) % 2 == 0:
-        early, came_refs = came_refs[0][:, pl.ds(place, width)], came_refs[1:]
+        early = came_refs.pop(0)[...]
     digit = (lax.axis_index(axis) // stride) % (len(came_refs) + 1)
     for k, came_ref in enumerate(came_refs, 1):
-        piece = jnp.where((digit ^ k) < digit, came_ref[:, pl.ds(place, width)].astype(F32), 0.0)
+        piece = jnp.where((digit ^ k) < digit, came_ref[...].astype(F32), 0.0)
         early = piece if early is None else early + piece
     for k in range(n):
-        held = early + bound_refs[k][:, pl.ds(place, width)]
-        if k & 1:
-            send_ref[k // 2] = held.astype(BF16)
+        held = early + bound_refs[k][...]
+        if k % 2 == 0:
+            outs[2 + k // 2][...] = held
+        elif k == 1:
+            outs[1][...] = held.astype(BF16)
         else:
-            keep_ref[k // 2] = held
+            outs[0][k // 2 - 1] = held.astype(BF16)
 
 
 def near(value):
@@ -216,11 +223,6 @@
 
 def far(value):
     return pltpu.with_memory_space_constraint(value, pltpu.HBM)
-
-
-def merged(held, got, bit):
-    kept = [k for k in held if not k & bit]
-    return {k: held[k] + got[i].astype(F32) for i, k in enumerate(kept)}
 
 
 def cost(flops, size):
@@ -277,33 +279,29 @@
         name="bounds",
     )(table, key, value)
 
-    parts, gate = [], None
+    onward, last, *keep = pl.pallas_call(
+        functools.partial(merge_kernel, "seqo", stride, n),
+        in_specs=[vmem] * (n + len(groups)),
+        out_specs=[vmem] * (n // 2 + 2),
+        out_shape=[pltpu.VMEM((n // 2 - 1, head, depth), BF16), pltpu.VMEM((head, depth), BF16)]
+        + [pltpu.VMEM((head, depth), F32)] * (n // 2),
+        compiler_params=params,
+        cost_estimate=cost(2 * n * head * depth, 8 * n * head * depth),
+        name="merge",
+    )(*bound, *(near(piece) for piece in groups))
+    held, last, bit = {2 * i: value for i, value in enumerate(keep)}, [last], 1
+    kept, held, landed = held[0], {k: value for k, value in held.items() if k}, []
+    while held:
+        handed = swap(onward, "seqi", bit)
+        landed.append(swap(last[0], "seqi", bit))
+        held = {k: value + handed[i].astype(F32) for i, (k, value) in enumerate(held.items())}
+        bit *= 2
+        last = [held.pop(bit).astype(BF16)]
+        more = [held.pop(k).astype(BF16) for k in list(held) if k & bit]
+        onward = jnp.stack(more) if more else None
+    final = []
     for c in range(CHUNKS):
-        send, keep = pl.pallas_call(
-            functools.partial(merge_kernel, "seqo", stride, c * chunk),
-            in_specs=[vmem] * (n + len(groups)),
-            out_specs=[vmem] * 2,
-            out_shape=[
-                pltpu.VMEM((n // 2, head, chunk), BF16),
-                pltpu.VMEM((n // 2, head, chunk), F32),
-            ],
-            compiler_params=params,
-            cost_estimate=cost(2 * n * head * chunk, 8 * n * head * chunk),
-            name="merge",
-        )(*bound, *(near(piece) for piece in groups))
-        got = swap(send, "seqi", 1)
-        parts.append(({k: keep[k // 2] for k in range(0, n, 2)}, got))
-    bit = 2
-    while bit < n:
-        for c, (held, got) in enumerate(parts):
-            if c > 0:
-                got, _ = lax.optimization_barrier((got, gate))
-            held = merged(held, got, bit // 2)
-            send = [held[k].astype(BF16) for k in held if k & bit]
-            gate = jnp.stack(send) if len(send) > 1 else send[0][None]
-            parts[c] = held, swap(gate, "seqi", bit)
-        bit *= 2
-    kept, last = [held[0] for held, _ in parts], [got[0] for _, got in parts]
+        final.append(swap(last[0][:, c * chunk : (c + 1) * chunk], "seqi", bit))
 
     query, local, tokens = [], [], None
     for c in range(CHUNKS):
@@ -331,15 +329,15 @@
         end = c == CHUNKS - 1
         total = [
             pl.pallas_call(
-                functools.partial(out_kernel, head, width, c * chunk, depth),
-                in_specs=[vmem] * (6 + len(total)),
+                functools.partial(out_kernel, head, width, c * chunk, depth, len(landed)),
+                in_specs=[vmem] * (6 + len(landed) + len(total)),
                 out_specs=hbm if end else vmem,
                 out_shape=shape((rows, depth), F32) if end else pltpu.VMEM((rows, depth), F32),
                 scratch_shapes=[pltpu.VMEM((rows, depth), F32), pltpu.SemaphoreType.DMA((steps,))] * end,
                 compiler_params=params,
                 cost_estimate=cost(2 * rows * depth * chunk, 2 * depth * chunk),
                 name="out",
-            )(query[c], local[c], kept[c], last[c], gain, w_out, *total)
+            )(query[c], local[c], gain, w_out, final[c], kept, *landed, *total)
         ]
     return total[0]
 

time: 43.1 us -> 41.9 us (0.972)
  the two profiles are of different devices: /device:TPU:0 before, /device:TPU:10 now
where the time goes in v3:
time: 41.9 us; the launch traced here: 41.7 us
  starting transfers between devices  17.4 us (42%)
  Pallas kernels  9.9 us (24%)
  waiting for transfers between devices  9.82 us (23%)
  local copies, waits for them, and re-layouts  4.42 us (11%)
    ppermute x10, starting transfers between devices, swap(): lax.ppermute(value, axis, [(i, i ^ bits) for i in range(lax.axis_size(axi...  17.4 us
    ppermute x10, waiting for transfers between devices, swap(): lax.ppermute(value, axis, [(i, i ^ bits) for i in range(lax.axis_size(axi...  9.82 us
    unnamed x24, local copies, waits for them, and re-layouts  4.41 us
    pallas_call x2, Pallas kernels, body(): pl.pallas_call(functools.partial(local_kernel, 'seqi', head, width, c * c...  3.46 us
    pallas_call x2, Pallas kernels, body(): pl.pallas_call(functools.partial(out_kernel, head, width, c * chunk, dept...  2.1 us
    pallas_call x1, Pallas kernels, body(): pl.pallas_call(functools.partial(state_kernel, head, width), in_specs=[vm...  1.5 us
    pallas_call x1, Pallas kernels, body(): pl.pallas_call(functools.partial(slot_kernel, 'seqi'), in_specs=[smem, vm...  1.35 us
    pallas_call x1, Pallas kernels, body(): pl.pallas_call(functools.partial(bound_kernel, 'seqi', head, width), in_s...  1.34 us
  transfers between devices with their start and end apart: 10, of which 4 were waited for; matrix products, arithmetic and copies ran while one was open for 0% of the time, Pallas kernels for 16%

profile of v3, /device:TPU:10, one launch (start us, length us, event | category | flops | bytes accessed | tf_op | source)
XLA Modules:
  0.0 41.7 jit_solution(15940634703404125076)
XLA Ops:
  0.0 0.0 copy-start
  0.0 1.6 %copy-done = bf16[1024,1024]{1,0:T(8,128)(2,1)S(1)} copy-done((bf16[1024,1024]{1,0:T(8,128)(2,1)S(1)}, bf16[1024,1024]{1,0:T(8,128)(2,1)}, u32[]{:S(2)}) %copy-start) | copy-done | bytes 2097176
  1.6 1.6 %copy-done.2 = bf16[1024,1024]{1,0:T(8,128)(2,1)S(1)} copy-done((bf16[1024,1024]{1,0:T(8,128)(2,1)S(1)}, bf16[1024,1024]{1,0:T(8,128)(2,1)}, u32[]{:S(2)}) %copy-start.2) | copy-done | bytes 2097176
  3.2 0.0 copy-start.6
  3.2 0.9 %copy-done.6 = bf16[128,1024]{1,0:T(8,128)(2,1)S(1)} copy-done((bf16[128,1024]{1,0:T(8,128)(2,1)S(1)}, bf16[128,1024]{1,0:T(8,128)(2,1)}, u32[]{:S(2)}) %copy-start.6) | copy-done | bytes 262168
  4.1 0.0 copy-start.10
  4.1 1.5 %states.1 = (bf16[128,1024]{1,0:T(8,128)(2,1)S(1)}, bf16[128,1024]{1,0:T(8,128)(2,1)S(1)}, bf16[64,1024]{1,0:T(8,128)(2,1)S(1)}) custom-call(bf16[128,1024]{1,0:T(8,128)(2,1)S(1)} %copy-done.6, bf16[1024,1024]{1,0:T(8,128)(2,1)S(1)} %copy-done, bf16[1024,1024]{1,0:T(8,128)(2,1)S(1)} %copy-done.2), custom_call_target="tpu_custom_call" | custom-call | flops 536870912 | bytes 4194304 | tf_op jit(solution)/shard_map/states/pallas_call | solution.py:261
  5.6 0.6 %collective-permute-start.3 = (bf16[64,1024]{1,0:T(8,128)(2,1)S(1)}, bf16[64,1024]{1,0:T(8,128)(2,1)S(1)}, u32[]{:S(2)}, u32[]{:S(2)}) collective-permute-start(bf16[64,1024]{1,0:T(8,128)(2,1)S(1)} %get-tuple-element.36), channel_id=1, source_target_pairs={{0,4},{4,0},{8,12},{12,8},{1,5},{5,1},{9,13},{13,9},{2,6},{6,2},{1... | collective-permute-start | bytes 393224 | tf_op jit(solution)/shard_map/ppermute | solution.py:179
  6.2 1.5 %collective-permute-start.4 = (bf16[64,1024]{1,0:T(8,128)(2,1)S(1)}, bf16[64,1024]{1,0:T(8,128)(2,1)S(1)}, u32[]{:S(2)}, u32[]{:S(2)}) collective-permute-start(bf16[64,1024]{1,0:T(8,128)(2,1)S(1)} %get-tuple-element.36), channel_id=1, source_target_pairs={{0,8},{4,12},{8,0},{12,4},{1,9},{5,13},{9,1},{13,5},{2,10},{6,14},... | collective-permute-start | bytes 393224 | tf_op jit(solution)/shard_map/ppermute | solution.py:179
  7.8 1.4 %collective-permute-start.5 = (bf16[64,1024]{1,0:T(8,128)(2,1)S(1)}, bf16[64,1024]{1,0:T(8,128)(2,1)S(1)}, u32[]{:S(2)}, u32[]{:S(2)}) collective-permute-start(bf16[64,1024]{1,0:T(8,128)(2,1)S(1)} %get-tuple-element.36), channel_id=1, source_target_pairs={{0,12},{4,8},{8,4},{12,0},{1,13},{5,9},{9,5},{13,1},{2,14},{6,10},... | collective-permute-start | bytes 393224 | tf_op jit(solution)/shard_map/ppermute | solution.py:179
  9.2 0.0 copy-done.10
  9.2 1.3 %bounds.1 = (f32[64,1024]{1,0:T(8,128)S(1)}, f32[64,1024]{1,0:T(8,128)S(1)}, f32[64,1024]{1,0:T(8,128)S(1)}, f32[64,1024]{1,0:T(8,128)S(1)}) custom-call(s32[1,4,2,4]{3,2,1,0:T(2,128)S(1)} %bitcast.8, bf16[128,1024]{1,0:T(8,128)(2,1)S(1)} %get-tuple-element.30.key_ref, bf16[128,1024]{1,0:T(8,128)(2,1)S(1)} %get-tuple-element.31.value_ref), custom_call_target="tpu_custom_call" | custom-call | flops 268435456 | bytes 524288 | tf_op jit(solution)/shard_map/bounds/pallas_call | solution.py:272
  10.5 1.5 %collective-permute-done.3.refs_4_ = bf16[64,1024]{1,0:T(8,128)(2,1)S(1)} collective-permute-done((bf16[64,1024]{1,0:T(8,128)(2,1)S(1)}, bf16[64,1024]{1,0:T(8,128)(2,1)S(1)}, u32[]{:S(2)}, u32[]{:S(2)}) %collective-permute-start.3) | collective-permute-done | bytes 131104 | tf_op jit(solution)/shard_map/ppermute | solution.py:179
  12.1 1.0 %collective-permute-done.4.refs_5_ = bf16[64,1024]{1,0:T(8,128)(2,1)S(1)} collective-permute-done((bf16[64,1024]{1,0:T(8,128)(2,1)S(1)}, bf16[64,1024]{1,0:T(8,128)(2,1)S(1)}, u32[]{:S(2)}, u32[]{:S(2)}) %collective-permute-start.4) | collective-permute-done | bytes 131104 | tf_op jit(solution)/shard_map/ppermute | solution.py:179
  13.1 1.6 %collective-permute-done.5.refs_6_ = bf16[64,1024]{1,0:T(8,128)(2,1)S(1)} collective-permute-done((bf16[64,1024]{1,0:T(8,128)(2,1)S(1)}, bf16[64,1024]{1,0:T(8,128)(2,1)S(1)}, u32[]{:S(2)}, u32[]{:S(2)}) %collective-permute-start.5) | collective-permute-done | bytes 131104 | tf_op jit(solution)/shard_map/ppermute | solution.py:179
  14.7 0.1 merge.1
  14.9 0.0 copy-start.7
  14.9 0.0 copy-start.8
  14.9 0.0 copy-start.11
  14.9 0.5 %collective-permute-start.6 = (bf16[1,64,1024]{2,1,0:T(8,128)(2,1)S(1)}, bf16[1,64,1024]{2,1,0:T(8,128)(2,1)S(1)}, u32[]{:S(2)}, u32[]{:S(2)}) collective-permute-start(bf16[1,64,1024]{2,1,0:T(8,128)(2,1)S(1)} %get-tuple-element.38), channel_id=1, source_target_pairs={{0,1},{1,0},{2,3},{3,2},{4,5},{5,4},{6,7},{7,6},{8,9},{9,8},{10,11... | collective-permute-start | bytes 393224 | tf_op jit(solution)/shard_map/ppermute | solution.py:179
  15.4 1.4 %slots.1 = (bf16[64,1024]{1,0:T(8,128)(2,1)S(1)}, bf16[64,1024]{1,0:T(8,128)(2,1)S(1)}, bf16[64,1024]{1,0:T(8,128)(2,1)S(1)}) custom-call(s32[1,4,2,4]{3,2,1,0:T(2,128)} %bitcast.7, bf16[128,1024]{1,0:T(8,128)(2,1)} %x_ref.3), custom_call_target="tpu_custom_call" | custom-call | flops 99999997952 | bytes 524288 | tf_op jit(solution)/shard_map/slots/pallas_call | solution.py:249
  16.8 1.6 %collective-permute-start = (bf16[64,1024]{1,0:T(8,128)(2,1)S(1)}, bf16[64,1024]{1,0:T(8,128)(2,1)S(1)}, u32[]{:S(2)}, u32[]{:S(2)}) collective-permute-start(bf16[64,1024]{1,0:T(8,128)(2,1)S(1)} %get-tuple-element.24), channel_id=1, source_target_pairs={{0,1},{1,0},{2,3},{3,2},{4,5},{5,4},{6,7},{7,6},{8,9},{9,8},{10,11... | collective-permute-start | bytes 393224 | tf_op jit(solution)/shard_map/ppermute | solution.py:179
  18.4 2.6 %collective-permute-start.1 = (bf16[64,1024]{1,0:T(8,128)(2,1)S(1)}, bf16[64,1024]{1,0:T(8,128)(2,1)S(1)}, u32[]{:S(2)}, u32[]{:S(2)}) collective-permute-start(bf16[64,1024]{1,0:T(8,128)(2,1)S(1)} %get-tuple-element.25), channel_id=1, source_target_pairs={{0,2},{1,3},{2,0},{3,1},{4,6},{5,7},{6,4},{7,5},{8,10},{9,11},{10,... | collective-permute-start | bytes 393224 | tf_op jit(solution)/shard_map/ppermute | solution.py:179
  21.0 0.0 collective-permute-start.2
  21.0 1.8 %collective-permute-start.8 = (bf16[64,1024]{1,0:T(8,128)(2,1)S(1)}, bf16[64,1024]{1,0:T(8,128)(2,1)S(1)}, u32[]{:S(2)}, u32[]{:S(2)}) collective-permute-start(bf16[64,1024]{1,0:T(8,128)(2,1)S(1)} %get-tuple-element.40), channel_id=1, source_target_pairs={{0,1},{1,0},{2,3},{3,2},{4,5},{5,4},{6,7},{7,6},{8,9},{9,8},{10,11... | collective-permute-start | bytes 393224 | tf_op jit(solution)/shard_map/ppermute | solution.py:179
  22.8 0.0 collective-permute-done.6
  22.9 1.8 %collective-permute-start.9 = (bf16[64,512]{1,0:T(8,128)(2,1)S(1)}, bf16[64,512]{1,0:T(8,128)(2,1)S(1)}, u32[]{:S(2)}, u32[]{:S(2)}) collective-permute-start(bf16[64,512]{1,0:T(8,128)(2,1)S(1)} %get-tuple-element.43), channel_id=1, source_target_pairs={{0,2},{1,3},{2,0},{3,1},{4,6},{5,7},{6,4},{7,5},{8,10},{9,11},{10,... | collective-permute-start | bytes 196616 | tf_op jit(solution)/shard_map/ppermute | solution.py:179
  24.6 0.0 collective-permute-done.refs_6_
  24.6 5.5 %collective-permute-start.7 = (bf16[64,512]{1,0:T(8,128)(2,1)S(1)}, bf16[64,512]{1,0:T(8,128)(2,1)S(1)}, u32[]{:S(2)}, u32[]{:S(2)}) collective-permute-start(bf16[64,512]{1,0:T(8,128)(2,1)S(1)} %get-tuple-element.44), channel_id=1, source_target_pairs={{0,2},{1,3},{2,0},{3,1},{4,6},{5,7},{6,4},{7,5},{8,10},{9,11},{10,... | collective-permute-start | bytes 196616 | tf_op jit(solution)/shard_map/ppermute | solution.py:179
  30.1 0.0 collective-permute-done.1.refs_7_
  30.1 5.6 %collective-permute-done.2.refs_8_ = bf16[64,1024]{1,0:T(8,128)(2,1)S(1)} collective-permute-done((bf16[64,1024]{1,0:T(8,128)(2,1)S(1)}, bf16[64,1024]{1,0:T(8,128)(2,1)S(1)}, u32[]{:S(2)}, u32[]{:S(2)}) %collective-permute-start.2) | collective-permute-done | bytes 131104 | tf_op jit(solution)/shard_map/ppermute | solution.py:179
  35.8 0.0 copy-done.7
  35.8 0.0 copy-done.8
  35.8 0.0 copy-done.11
  35.8 0.0 copy-done.1
  35.8 0.0 copy-done.3
  35.8 0.0 copy-done.4
  35.8 2.1 %local.2 = (bf16[128,512]{1,0:T(8,128)(2,1)S(1)}, f32[128,512]{1,0:T(8,128)S(1)}, bf16[128,1024]{1,0:T(8,128)(2,1)S(1)}) custom-call(s32[1,4,2,4]{3,2,1,0:T(2,128)S(1)} %bitcast.9, s32[1,64,64]{2,1,0:T(8,128)S(1)} %copy-done.8, bf16[128,1024]{1,0:T(8,128)(2,1)S(1)} %copy-done.7, bf16[1024,1024]{1,0:T(8,128)(2,1)S(1)} %copy-done.4, ...), custom_call_target="tpu_custom_call" | custom-call | flops 402653184 | bytes 3145728 | tf_op jit(solution)/shard_map/local/pallas_call | solution.py:314
  38.0 0.0 copy-start.5
  38.0 0.0 copy-start.9
  38.0 1.3 %local.3 = (bf16[128,512]{1,0:T(8,128)(2,1)S(1)}, f32[128,512]{1,0:T(8,128)S(1)}) custom-call(s32[1,64,64]{2,1,0:T(8,128)S(1)} %copy-done.8, bf16[128,1024]{1,0:T(8,128)(2,1)S(1)} %get-tuple-element.27.refs_1_, bf16[1024,1024]{1,0:T(8,128)(2,1)S(1)} %copy-done.4, bf16[1024,1024]{1,0:T(8,128)(2,1)S(1)} %copy-done.1, bf16[1024,1024]{1,0:T(8,128)(2,1)S(1)} %copy-done.3), custom_call_target="tpu_custom_call" | custom-call | flops 402653184 | bytes 3145728 | tf_op jit(solution)/shard_map/local/pallas_call | solution.py:314
  39.3 0.0 collective-permute-done.8.rest_0_
  39.3 0.0 collective-permute-done.9.final_ref
  39.3 0.2 copy-done.5
  39.6 0.0 copy-done.9
  39.6 0.7 %out.2.rest_1_ = f32[128,1024]{1,0:T(8,128)S(1)} custom-call(bf16[128,512]{1,0:T(8,128)(2,1)S(1)} %get-tuple-element.41.q_ref, f32[128,512]{1,0:T(8,128)S(1)} %get-tuple-element.42.local_ref, f32[1,1024]{1,0:T(1,128)S(1)} %bitcast.5, bf16[1024,1024]{1,0:T(8,128)(2,1)S(1)} %copy-done.5, bf16[64,512]{1,0:T(8,128)(2,1)S(1)} %collective-permute-done.9.final_ref, ...), custom_call_target="tpu_custom_call" | custom-call | flops 134217728 | bytes 1048576 | tf_op jit(solution)/shard_map/out/pallas_call | solution.py:331
  40.3 0.0 collective-permute-done.7.final_ref
  40.3 1.4 %out.3 = f32[128,1024]{1,0:T(8,128)} custom-call(bf16[128,512]{1,0:T(8,128)(2,1)S(1)} %get-tuple-element.28.q_ref, f32[128,512]{1,0:T(8,128)S(1)} %get-tuple-element.29.local_ref, f32[1,1024]{1,0:T(1,128)S(1)} %bitcast.6, bf16[1024,1024]{1,0:T(8,128)(2,1)S(1)} %copy-done.5, bf16[64,512]{1,0:T(8,128)(2,1)S(1)} %collective-permute-done.7.final_ref, ...), custom_call_target="tpu_custom_call" | custom-call | flops 134217728 | bytes 1048576 | tf_op jit(solution)/shard_map/out/pallas_call | solution.py:331
  (6 shorter events, 0.0 us)
Async XLA Ops:
  0.0 1.6 %copy-start = (bf16[1024,1024]{1,0:T(8,128)(2,1)S(1)}, bf16[1024,1024]{1,0:T(8,128)(2,1)}, u32[]{:S(2)}) copy-start(bf16[1024,1024]{1,0:T(8,128)(2,1)} %wk.1) | copy-start | bytes 6291460
  1.6 1.6 %copy-start.2 = (bf16[1024,1024]{1,0:T(8,128)(2,1)S(1)}, bf16[1024,1024]{1,0:T(8,128)(2,1)}, u32[]{:S(2)}) copy-start(bf16[1024,1024]{1,0:T(8,128)(2,1)} %wv.1) | copy-start | bytes 6291460
  3.2 0.9 %copy-start.6 = (bf16[128,1024]{1,0:T(8,128)(2,1)S(1)}, bf16[128,1024]{1,0:T(8,128)(2,1)}, u32[]{:S(2)}) copy-start(bf16[128,1024]{1,0:T(8,128)(2,1)} %x_ref.3) | copy-start | bytes 786436
  4.1 5.1 %copy-start.10 = (s32[1,4,4,2]{2,3,1,0:T(2,128)S(1)}, s32[1,4,4,2]{2,3,1,0:T(2,128)}, u32[]{:S(2)}) copy-start(s32[1,4,4,2]{2,3,1,0:T(2,128)} %param.9) | copy-start | bytes 388
  5.6 6.4 %collective-permute-start.3 = (bf16[64,1024]{1,0:T(8,128)(2,1)S(1)}, bf16[64,1024]{1,0:T(8,128)(2,1)S(1)}, u32[]{:S(2)}, u32[]{:S(2)}) collective-permute-start(bf16[64,1024]{1,0:T(8,128)(2,1)S(1)} %get-tuple-element.36), channel_id=1, source_target_pairs={{0,4},{4,0},{8,12},{12,8},{1,5},{5,1},{9,13},{13,9},{2,6},{6,2},{1... | collective-permute-start | bytes 393224 | tf_op jit(solution)/shard_map/ppermute | solution.py:179
  6.2 6.8 %collective-permute-start.4 = (bf16[64,1024]{1,0:T(8,128)(2,1)S(1)}, bf16[64,1024]{1,0:T(8,128)(2,1)S(1)}, u32[]{:S(2)}, u32[]{:S(2)}) collective-permute-start(bf16[64,1024]{1,0:T(8,128)(2,1)S(1)} %get-tuple-element.36), channel_id=1, source_target_pairs={{0,8},{4,12},{8,0},{12,4},{1,9},{5,13},{9,1},{13,5},{2,10},{6,14},... | collective-permute-start | bytes 393224 | tf_op jit(solution)/shard_map/ppermute | solution.py:179
  7.8 6.9 %collective-permute-start.5 = (bf16[64,1024]{1,0:T(8,128)(2,1)S(1)}, bf16[64,1024]{1,0:T(8,128)(2,1)S(1)}, u32[]{:S(2)}, u32[]{:S(2)}) collective-permute-start(bf16[64,1024]{1,0:T(8,128)(2,1)S(1)} %get-tuple-element.36), channel_id=1, source_target_pairs={{0,12},{4,8},{8,4},{12,0},{1,13},{5,9},{9,5},{13,1},{2,14},{6,10},... | collective-permute-start | bytes 393224 | tf_op jit(solution)/shard_map/ppermute | solution.py:179
  14.9 20.9 %copy-start.7 = (bf16[128,1024]{1,0:T(8,128)(2,1)S(1)}, bf16[128,1024]{1,0:T(8,128)(2,1)}, u32[]{:S(2)}) copy-start(bf16[128,1024]{1,0:T(8,128)(2,1)} %x_ref.3) | copy-start | bytes 786436
  14.9 20.9 %copy-start.8 = (s32[1,64,64]{2,1,0:T(8,128)S(1)}, s32[1,64,64]{2,1,0:T(8,128)}, u32[]{:S(2)}) copy-start(s32[1,64,64]{2,1,0:T(8,128)} %refs_0_.1) | copy-start | bytes 49156
  14.9 20.9 %copy-start.11 = (s32[1,4,4,2]{2,3,1,0:T(2,128)S(1)}, s32[1,4,4,2]{2,3,1,0:T(2,128)}, u32[]{:S(2)}) copy-start(s32[1,4,4,2]{2,3,1,0:T(2,128)} %param.9) | copy-start | bytes 388
  14.9 7.9 %collective-permute-start.6 = (bf16[1,64,1024]{2,1,0:T(8,128)(2,1)S(1)}, bf16[1,64,1024]{2,1,0:T(8,128)(2,1)S(1)}, u32[]{:S(2)}, u32[]{:S(2)}) collective-permute-start(bf16[1,64,1024]{2,1,0:T(8,128)(2,1)S(1)} %get-tuple-element.38), channel_id=1, source_target_pairs={{0,1},{1,0},{2,3},{3,2},{4,5},{5,4},{6,7},{7,6},{8,9},{9,8},{10,11... | collective-permute-start | bytes 393224 | tf_op jit(solution)/shard_map/ppermute | solution.py:179
  15.4 20.4 %copy-start.1 = (bf16[1024,1024]{1,0:T(8,128)(2,1)S(1)}, bf16[1024,1024]{1,0:T(8,128)(2,1)}, u32[]{:S(2)}) copy-start(bf16[1024,1024]{1,0:T(8,128)(2,1)} %wk.1) | copy-start | bytes 6291460
  15.4 20.4 %copy-start.3 = (bf16[1024,1024]{1,0:T(8,128)(2,1)S(1)}, bf16[1024,1024]{1,0:T(8,128)(2,1)}, u32[]{:S(2)}) copy-start(bf16[1024,1024]{1,0:T(8,128)(2,1)} %wv.1) | copy-start | bytes 6291460
  15.4 20.4 %copy-start.4 = (bf16[1024,1024]{1,0:T(8,128)(2,1)S(1)}, bf16[1024,1024]{1,0:T(8,128)(2,1)}, u32[]{:S(2)}) copy-start(bf16[1024,1024]{1,0:T(8,128)(2,1)} %refs_2_.3) | copy-start | bytes 6291460
  16.8 7.8 %collective-permute-start = (bf16[64,1024]{1,0:T(8,128)(2,1)S(1)}, bf16[64,1024]{1,0:T(8,128)(2,1)S(1)}, u32[]{:S(2)}, u32[]{:S(2)}) collective-permute-start(bf16[64,1024]{1,0:T(8,128)(2,1)S(1)} %get-tuple-element.24), channel_id=1, source_target_pairs={{0,1},{1,0},{2,3},{3,2},{4,5},{5,4},{6,7},{7,6},{8,9},{9,8},{10,11... | collective-permute-start | bytes 393224 | tf_op jit(solution)/shard_map/ppermute | solution.py:179
  18.4 11.7 %collective-permute-start.1 = (bf16[64,1024]{1,0:T(8,128)(2,1)S(1)}, bf16[64,1024]{1,0:T(8,128)(2,1)S(1)}, u32[]{:S(2)}, u32[]{:S(2)}) collective-permute-start(bf16[64,1024]{1,0:T(8,128)(2,1)S(1)} %get-tuple-element.25), channel_id=1, source_target_pairs={{0,2},{1,3},{2,0},{3,1},{4,6},{5,7},{6,4},{7,5},{8,10},{9,11},{10,... | collective-permute-start | bytes 393224 | tf_op jit(solution)/shard_map/ppermute | solution.py:179
  21.0 14.8 %collective-permute-start.2 = (bf16[64,1024]{1,0:T(8,128)(2,1)S(1)}, bf16[64,1024]{1,0:T(8,128)(2,1)S(1)}, u32[]{:S(2)}, u32[]{:S(2)}) collective-permute-start(bf16[64,1024]{1,0:T(8,128)(2,1)S(1)} %get-tuple-element.26), channel_id=1, source_target_pairs={{0,3},{1,2},{2,1},{3,0},{4,7},{5,6},{6,5},{7,4},{8,11},{9,10},{10,... | collective-permute-start | bytes 393224 | tf_op jit(solution)/shard_map/ppermute | solution.py:179
  21.0 18.3 %collective-permute-start.8 = (bf16[64,1024]{1,0:T(8,128)(2,1)S(1)}, bf16[64,1024]{1,0:T(8,128)(2,1)S(1)}, u32[]{:S(2)}, u32[]{:S(2)}) collective-permute-start(bf16[64,1024]{1,0:T(8,128)(2,1)S(1)} %get-tuple-element.40), channel_id=1, source_target_pairs={{0,1},{1,0},{2,3},{3,2},{4,5},{5,4},{6,7},{7,6},{8,9},{9,8},{10,11... | collective-permute-start | bytes 393224 | tf_op jit(solution)/shard_map/ppermute | solution.py:179
  22.9 16.5 %collective-permute-start.9 = (bf16[64,512]{1,0:T(8,128)(2,1)S(1)}, bf16[64,512]{1,0:T(8,128)(2,1)S(1)}, u32[]{:S(2)}, u32[]{:S(2)}) collective-permute-start(bf16[64,512]{1,0:T(8,128)(2,1)S(1)} %get-tuple-element.43), channel_id=1, source_target_pairs={{0,2},{1,3},{2,0},{3,1},{4,6},{5,7},{6,4},{7,5},{8,10},{9,11},{10,... | collective-permute-start | bytes 196616 | tf_op jit(solution)/shard_map/ppermute | solution.py:179
  24.6 15.6 %collective-permute-start.7 = (bf16[64,512]{1,0:T(8,128)(2,1)S(1)}, bf16[64,512]{1,0:T(8,128)(2,1)S(1)}, u32[]{:S(2)}, u32[]{:S(2)}) collective-permute-start(bf16[64,512]{1,0:T(8,128)(2,1)S(1)} %get-tuple-element.44), channel_id=1, source_target_pairs={{0,2},{1,3},{2,0},{3,1},{4,6},{5,7},{6,4},{7,5},{8,10},{9,11},{10,... | collective-permute-start | bytes 196616 | tf_op jit(solution)/shard_map/ppermute | solution.py:179
  38.0 1.6 %copy-start.5 = (bf16[1024,1024]{1,0:T(8,128)(2,1)S(1)}, bf16[1024,1024]{1,0:T(8,128)(2,1)}, u32[]{:S(2)}) copy-start(bf16[1024,1024]{1,0:T(8,128)(2,1)} %w.3) | copy-start | bytes 6291460
  38.0 1.6 %copy-start.9 = (f32[1024]{0:T(1024)S(1)}, f32[1024]{0:T(1024)}, u32[]{:S(2)}) copy-start(f32[1024]{0:T(1024)} %param.14) | copy-start | bytes 12292

commit v4 on v3

--- a/solution.py
+++ b/solution.py
@@ -132,27 +132,38 @@
         q_ref[:, inner] = query
 
 
-def out_kernel(head, width, place, depth, steps, q_ref, local_ref, gain_ref, w, final_ref, kept_ref, *rest):
+def spread(part, heads, same):
+    return jnp.where(same, jnp.concatenate([part] * heads, axis=0), jnp.zeros(same.shape, BF16))
+
+
+def carry_kernel(head, width, chunks, kept_ref, *refs):
+    queries, locals_, landed, outs = refs[:chunks], refs[chunks : 2 * chunks], refs[2 * chunks : -chunks], refs[-chunks:]
+    same = iota((width, width), 0) // head == iota((width, width), 1) // head
+    chunk = outs[0].shape[1]
+    for j in range(kept_ref.shape[1] // width):
+        c, place = divmod(j * width, chunk)
+        cols, inner = pl.ds(j * width, width), pl.ds(place, width)
+        prefix = kept_ref[:, cols]
+        for ref in landed:
+            prefix = prefix + ref[:, cols].astype(F32)
+        high = prefix.astype(BF16)
+        low = (prefix - high.astype(F32)).astype(BF16)
+        attended = locals_[c][:, inner]
+        for part in (high, low):
+            attended = attended + mm(queries[c][:, inner], spread(part, width // head, same))
+        outs[c][:, inner] = attended
+
+
+def out_kernel(head, width, place, depth, q_ref, local_ref, gain_ref, w, final_ref, *rest):
     chunk = final_ref.shape[1]
-    landed, rest = rest[:steps], rest[steps:]
     so_far, rest = (rest[0], rest[1:]) if place > 0 else (None, rest)
     heads = width // head
     same = iota((width, width), 0) // head == iota((width, width), 1) // head
     ones = same.astype(BF16)
-    zero = jnp.zeros((width, width), BF16)
     normed = []
     for j in range(chunk // width):
         inner, cols = pl.ds(j * width, width), pl.ds(place + j * width, width)
-        prefix = kept_ref[:, cols] + final_ref[:, inner].astype(F32)
-        for ref in landed:
-            prefix = prefix + ref[:, cols].astype(F32)
-        high = prefix.astype(BF16)
-        low = (prefix - high.astype(F32)).astype(BF16)
-        query = q_ref[:, inner]
-        attended = local_ref[:, inner]
-        for part in (high, low):
-            spread = jnp.where(same, jnp.concatenate([part] * heads, axis=0), zero)
-            attended = attended + mm(query, spread)
+        attended = local_ref[:, inner] + mm(q_ref[:, inner], spread(final_ref[:, inner], heads, same))
         square = attended * attended
         sq_high = square.astype(BF16)
         sq_low = (square - sq_high.astype(F32)).astype(BF16)
@@ -324,20 +335,29 @@
         local.append(local_part)
         tokens = rest[0] if rest else tokens
 
+    local = pl.pallas_call(
+        functools.partial(carry_kernel, head, width, CHUNKS),
+        in_specs=[vmem] * (1 + 2 * CHUNKS + len(landed)),
+        out_specs=[vmem] * CHUNKS,
+        out_shape=[pltpu.VMEM((rows, chunk), F32)] * CHUNKS,
+        compiler_params=params,
+        cost_estimate=cost(4 * rows * depth * width, 8 * rows * depth),
+        name="carry",
+    )(kept, *query, *local, *landed)
     gain, total = norm_gain.reshape(1, depth), []
     for c in range(CHUNKS):
         end = c == CHUNKS - 1
         total = [
             pl.pallas_call(
-                functools.partial(out_kernel, head, width, c * chunk, depth, len(landed)),
-                in_specs=[vmem] * (6 + len(landed) + len(total)),
+                functools.partial(out_kernel, head, width, c * chunk, depth),
+                in_specs=[vmem] * (5 + len(total)),
                 out_specs=hbm if end else vmem,
                 out_shape=shape((rows, depth), F32) if end else pltpu.VMEM((rows, depth), F32),
                 scratch_shapes=[pltpu.VMEM((rows, depth), F32), pltpu.SemaphoreType.DMA((steps,))] * end,
                 compiler_params=params,
                 cost_estimate=cost(2 * rows * depth * chunk, 2 * depth * chunk),
                 name="out",
-            )(query[c], local[c], gain, w_out, final[c], kept, *landed, *total)
+            )(query[c], local[c], gain, w_out, final[c], *total)
         ]
     return total[0]
 

time: 41.9 us -> 41.9 us (level)
  transfers between devices with their start and end apart: 10 -> 10, of which waited for: 4 -> 4; matrix products, arithmetic and copies ran while one was open for 0% -> 0% of each run, Pallas kernels for 16% -> 17%
where the time goes in v4:
time: 41.9 us; the launch traced here: 41.7 us
  starting transfers between devices  17.4 us (42%)
  Pallas kernels  10.1 us (24%)
  waiting for transfers between devices  9.82 us (23%)
  local copies, waits for them, and re-layouts  4.19 us (10%)
    ppermute x10, starting transfers between devices, swap(): lax.ppermute(value, axis, [(i, i ^ bits) for i in range(lax.axis_size(axi...  17.4 us
    ppermute x10, waiting for transfers between devices, swap(): lax.ppermute(value, axis, [(i, i ^ bits) for i in range(lax.axis_size(axi...  9.82 us
    unnamed x24, local copies, waits for them, and re-layouts  4.18 us
    pallas_call x2, Pallas kernels, body(): pl.pallas_call(functools.partial(local_kernel, 'seqi', head, width, c * c...  3.46 us
    pallas_call x2, Pallas kernels, body(): pl.pallas_call(functools.partial(out_kernel, head, width, c * chunk, dept...  2.01 us
    pallas_call x1, Pallas kernels, body(): pl.pallas_call(functools.partial(state_kernel, head, width), in_specs=[vm...  1.5 us
    pallas_call x1, Pallas kernels, body(): pl.pallas_call(functools.partial(slot_kernel, 'seqi'), in_specs=[smem, vm...  1.35 us
    pallas_call x1, Pallas kernels, body(): pl.pallas_call(functools.partial(bound_kernel, 'seqi', head, width), in_s...  1.34 us
  transfers between devices with their start and end apart: 10, of which 4 were waited for; matrix products, arithmetic and copies ran while one was open for 0% of the time, Pallas kernels for 17%

profile of v4, /device:TPU:10, one launch (start us, length us, event | category | flops | bytes accessed | tf_op | source)
XLA Modules:
  0.0 41.7 jit_solution(11307734472512709563)
XLA Ops:
  0.0 0.0 copy-start
  0.0 1.6 %copy-done = bf16[1024,1024]{1,0:T(8,128)(2,1)S(1)} copy-done((bf16[1024,1024]{1,0:T(8,128)(2,1)S(1)}, bf16[1024,1024]{1,0:T(8,128)(2,1)}, u32[]{:S(2)}) %copy-start) | copy-done | bytes 2097176
  1.6 1.6 %copy-done.2 = bf16[1024,1024]{1,0:T(8,128)(2,1)S(1)} copy-done((bf16[1024,1024]{1,0:T(8,128)(2,1)S(1)}, bf16[1024,1024]{1,0:T(8,128)(2,1)}, u32[]{:S(2)}) %copy-start.2) | copy-done | bytes 2097176
  3.2 0.0 copy-start.6
  3.2 0.9 %copy-done.6 = bf16[128,1024]{1,0:T(8,128)(2,1)S(1)} copy-done((bf16[128,1024]{1,0:T(8,128)(2,1)S(1)}, bf16[128,1024]{1,0:T(8,128)(2,1)}, u32[]{:S(2)}) %copy-start.6) | copy-done | bytes 262168
  4.1 1.5 %states.1 = (bf16[128,1024]{1,0:T(8,128)(2,1)S(1)}, bf16[128,1024]{1,0:T(8,128)(2,1)S(1)}, bf16[64,1024]{1,0:T(8,128)(2,1)S(1)}) custom-call(bf16[128,1024]{1,0:T(8,128)(2,1)S(1)} %copy-done.6, bf16[1024,1024]{1,0:T(8,128)(2,1)S(1)} %copy-done, bf16[1024,1024]{1,0:T(8,128)(2,1)S(1)} %copy-done.2), custom_call_target="tpu_custom_call" | custom-call | flops 536870912 | bytes 4194304 | tf_op jit(solution)/shard_map/states/pallas_call | solution.py:272
  5.6 0.6 %collective-permute-start.3 = (bf16[64,1024]{1,0:T(8,128)(2,1)S(1)}, bf16[64,1024]{1,0:T(8,128)(2,1)S(1)}, u32[]{:S(2)}, u32[]{:S(2)}) collective-permute-start(bf16[64,1024]{1,0:T(8,128)(2,1)S(1)} %get-tuple-element.37), channel_id=1, source_target_pairs={{0,4},{4,0},{8,12},{12,8},{1,5},{5,1},{9,13},{13,9},{2,6},{6,2},{1... | collective-permute-start | bytes 393224 | tf_op jit(solution)/shard_map/ppermute | solution.py:190
  6.2 1.5 %collective-permute-start.4 = (bf16[64,1024]{1,0:T(8,128)(2,1)S(1)}, bf16[64,1024]{1,0:T(8,128)(2,1)S(1)}, u32[]{:S(2)}, u32[]{:S(2)}) collective-permute-start(bf16[64,1024]{1,0:T(8,128)(2,1)S(1)} %get-tuple-element.37), channel_id=1, source_target_pairs={{0,8},{4,12},{8,0},{12,4},{1,9},{5,13},{9,1},{13,5},{2,10},{6,14},... | collective-permute-start | bytes 393224 | tf_op jit(solution)/shard_map/ppermute | solution.py:190
  7.8 1.4 %collective-permute-start.5 = (bf16[64,1024]{1,0:T(8,128)(2,1)S(1)}, bf16[64,1024]{1,0:T(8,128)(2,1)S(1)}, u32[]{:S(2)}, u32[]{:S(2)}) collective-permute-start(bf16[64,1024]{1,0:T(8,128)(2,1)S(1)} %get-tuple-element.37), channel_id=1, source_target_pairs={{0,12},{4,8},{8,4},{12,0},{1,13},{5,9},{9,5},{13,1},{2,14},{6,10},... | collective-permute-start | bytes 393224 | tf_op jit(solution)/shard_map/ppermute | solution.py:190
  9.2 0.0 copy-done.10
  9.2 1.3 %bounds.1 = (f32[64,1024]{1,0:T(8,128)S(1)}, f32[64,1024]{1,0:T(8,128)S(1)}, f32[64,1024]{1,0:T(8,128)S(1)}, f32[64,1024]{1,0:T(8,128)S(1)}) custom-call(s32[1,4,2,4]{3,2,1,0:T(2,128)S(1)} %bitcast.8, bf16[128,1024]{1,0:T(8,128)(2,1)S(1)} %get-tuple-element.31.key_ref, bf16[128,1024]{1,0:T(8,128)(2,1)S(1)} %get-tuple-element.32.value_ref), custom_call_target="tpu_custom_call" | custom-call | flops 268435456 | bytes 524288 | tf_op jit(solution)/shard_map/bounds/pallas_call | solution.py:283
  10.5 1.5 %collective-permute-done.3.refs_4_ = bf16[64,1024]{1,0:T(8,128)(2,1)S(1)} collective-permute-done((bf16[64,1024]{1,0:T(8,128)(2,1)S(1)}, bf16[64,1024]{1,0:T(8,128)(2,1)S(1)}, u32[]{:S(2)}, u32[]{:S(2)}) %collective-permute-start.3) | collective-permute-done | bytes 131104 | tf_op jit(solution)/shard_map/ppermute | solution.py:190
  12.1 1.0 %collective-permute-done.4.refs_5_ = bf16[64,1024]{1,0:T(8,128)(2,1)S(1)} collective-permute-done((bf16[64,1024]{1,0:T(8,128)(2,1)S(1)}, bf16[64,1024]{1,0:T(8,128)(2,1)S(1)}, u32[]{:S(2)}, u32[]{:S(2)}) %collective-permute-start.4) | collective-permute-done | bytes 131104 | tf_op jit(solution)/shard_map/ppermute | solution.py:190
  13.1 1.6 %collective-permute-done.5.refs_6_ = bf16[64,1024]{1,0:T(8,128)(2,1)S(1)} collective-permute-done((bf16[64,1024]{1,0:T(8,128)(2,1)S(1)}, bf16[64,1024]{1,0:T(8,128)(2,1)S(1)}, u32[]{:S(2)}, u32[]{:S(2)}) %collective-permute-start.5) | collective-permute-done | bytes 131104 | tf_op jit(solution)/shard_map/ppermute | solution.py:190
  14.7 0.1 merge.1
  14.9 0.0 copy-start.7
  14.9 0.0 copy-start.8
  14.9 0.0 copy-start.11
  14.9 0.5 %collective-permute-start.7 = (bf16[1,64,1024]{2,1,0:T(8,128)(2,1)S(1)}, bf16[1,64,1024]{2,1,0:T(8,128)(2,1)S(1)}, u32[]{:S(2)}, u32[]{:S(2)}) collective-permute-start(bf16[1,64,1024]{2,1,0:T(8,128)(2,1)S(1)} %get-tuple-element.45), channel_id=1, source_target_pairs={{0,1},{1,0},{2,3},{3,2},{4,5},{5,4},{6,7},{7,6},{8,9},{9,8},{10,11... | collective-permute-start | bytes 393224 | tf_op jit(solution)/shard_map/ppermute | solution.py:190
  15.4 1.4 %slots.1 = (bf16[64,1024]{1,0:T(8,128)(2,1)S(1)}, bf16[64,1024]{1,0:T(8,128)(2,1)S(1)}, bf16[64,1024]{1,0:T(8,128)(2,1)S(1)}) custom-call(s32[1,4,2,4]{3,2,1,0:T(2,128)} %bitcast.7, bf16[128,1024]{1,0:T(8,128)(2,1)} %x_ref.3), custom_call_target="tpu_custom_call" | custom-call | flops 99999997952 | bytes 524288 | tf_op jit(solution)/shard_map/slots/pallas_call | solution.py:260
  16.8 1.6 %collective-permute-start = (bf16[64,1024]{1,0:T(8,128)(2,1)S(1)}, bf16[64,1024]{1,0:T(8,128)(2,1)S(1)}, u32[]{:S(2)}, u32[]{:S(2)}) collective-permute-start(bf16[64,1024]{1,0:T(8,128)(2,1)S(1)} %get-tuple-element.26), channel_id=1, source_target_pairs={{0,1},{1,0},{2,3},{3,2},{4,5},{5,4},{6,7},{7,6},{8,9},{9,8},{10,11... | collective-permute-start | bytes 393224 | tf_op jit(solution)/shard_map/ppermute | solution.py:190
  18.4 2.6 %collective-permute-start.1 = (bf16[64,1024]{1,0:T(8,128)(2,1)S(1)}, bf16[64,1024]{1,0:T(8,128)(2,1)S(1)}, u32[]{:S(2)}, u32[]{:S(2)}) collective-permute-start(bf16[64,1024]{1,0:T(8,128)(2,1)S(1)} %get-tuple-element.27), channel_id=1, source_target_pairs={{0,2},{1,3},{2,0},{3,1},{4,6},{5,7},{6,4},{7,5},{8,10},{9,11},{10,... | collective-permute-start | bytes 393224 | tf_op jit(solution)/shard_map/ppermute | solution.py:190
  21.0 0.0 collective-permute-start.2
  21.0 1.8 %collective-permute-start.6 = (bf16[64,1024]{1,0:T(8,128)(2,1)S(1)}, bf16[64,1024]{1,0:T(8,128)(2,1)S(1)}, u32[]{:S(2)}, u32[]{:S(2)}) collective-permute-start(bf16[64,1024]{1,0:T(8,128)(2,1)S(1)} %get-tuple-element.42), channel_id=1, source_target_pairs={{0,1},{1,0},{2,3},{3,2},{4,5},{5,4},{6,7},{7,6},{8,9},{9,8},{10,11... | collective-permute-start | bytes 393224 | tf_op jit(solution)/shard_map/ppermute | solution.py:190
  22.8 0.0 collective-permute-done.7
  22.9 1.8 %collective-permute-start.9 = (bf16[64,512]{1,0:T(8,128)(2,1)S(1)}, bf16[64,512]{1,0:T(8,128)(2,1)S(1)}, u32[]{:S(2)}, u32[]{:S(2)}) collective-permute-start(bf16[64,512]{1,0:T(8,128)(2,1)S(1)} %get-tuple-element.47), channel_id=1, source_target_pairs={{0,2},{1,3},{2,0},{3,1},{4,6},{5,7},{6,4},{7,5},{8,10},{9,11},{10,... | collective-permute-start | bytes 196616 | tf_op jit(solution)/shard_map/ppermute | solution.py:190
  24.6 0.0 collective-permute-done.refs_6_
  24.6 5.5 %collective-permute-start.8 = (bf16[64,512]{1,0:T(8,128)(2,1)S(1)}, bf16[64,512]{1,0:T(8,128)(2,1)S(1)}, u32[]{:S(2)}, u32[]{:S(2)}) collective-permute-start(bf16[64,512]{1,0:T(8,128)(2,1)S(1)} %get-tuple-element.48), channel_id=1, source_target_pairs={{0,2},{1,3},{2,0},{3,1},{4,6},{5,7},{6,4},{7,5},{8,10},{9,11},{10,... | collective-permute-start | bytes 196616 | tf_op jit(solution)/shard_map/ppermute | solution.py:190
  30.1 0.0 collective-permute-done.1.refs_7_
  30.1 5.6 %collective-permute-done.2.refs_8_ = bf16[64,1024]{1,0:T(8,128)(2,1)S(1)} collective-permute-done((bf16[64,1024]{1,0:T(8,128)(2,1)S(1)}, bf16[64,1024]{1,0:T(8,128)(2,1)S(1)}, u32[]{:S(2)}, u32[]{:S(2)}) %collective-permute-start.2) | collective-permute-done | bytes 131104 | tf_op jit(solution)/shard_map/ppermute | solution.py:190
  35.8 0.0 copy-done.7
  35.8 0.0 copy-done.8
  35.8 0.0 copy-done.11
  35.8 0.0 copy-done.1
  35.8 0.0 copy-done.3
  35.8 0.0 copy-done.4
  35.8 2.1 %local.2 = (bf16[128,512]{1,0:T(8,128)(2,1)S(1)}, f32[128,512]{1,0:T(8,128)S(1)}, bf16[128,1024]{1,0:T(8,128)(2,1)S(1)}) custom-call(s32[1,4,2,4]{3,2,1,0:T(2,128)S(1)} %bitcast.9, s32[1,64,64]{2,1,0:T(8,128)S(1)} %copy-done.8, bf16[128,1024]{1,0:T(8,128)(2,1)S(1)} %copy-done.7, bf16[1024,1024]{1,0:T(8,128)(2,1)S(1)} %copy-done.4, ...), custom_call_target="tpu_custom_call" | custom-call | flops 402653184 | bytes 3145728 | tf_op jit(solution)/shard_map/local/pallas_call | solution.py:325
  38.0 0.0 copy-start.5
  38.0 0.0 copy-start.9
  38.0 1.3 %local.3 = (bf16[128,512]{1,0:T(8,128)(2,1)S(1)}, f32[128,512]{1,0:T(8,128)S(1)}) custom-call(s32[1,64,64]{2,1,0:T(8,128)S(1)} %copy-done.8, bf16[128,1024]{1,0:T(8,128)(2,1)S(1)} %get-tuple-element.29.refs_1_, bf16[1024,1024]{1,0:T(8,128)(2,1)S(1)} %copy-done.4, bf16[1024,1024]{1,0:T(8,128)(2,1)S(1)} %copy-done.1, bf16[1024,1024]{1,0:T(8,128)(2,1)S(1)} %copy-done.3), custom_call_target="tpu_custom_call" | custom-call | flops 402653184 | bytes 3145728 | tf_op jit(solution)/shard_map/local/pallas_call | solution.py:325
  39.3 0.0 collective-permute-done.6.refs_4_
  39.3 0.3 carry.1
  39.7 0.0 collective-permute-done.9.final_ref
  39.7 0.0 copy-done.5
  39.7 0.0 copy-done.9
  39.7 0.6 %out.2.rest_0_ = f32[128,1024]{1,0:T(8,128)S(1)} custom-call(bf16[128,512]{1,0:T(8,128)(2,1)S(1)} %get-tuple-element.39.refs_0_.q_ref, f32[128,512]{1,0:T(8,128)S(1)} %get-tuple-element.46.local_ref, f32[1,1024]{1,0:T(1,128)S(1)} %bitcast.5, bf16[1024,1024]{1,0:T(8,128)(2,1)S(1)} %copy-done.5, bf16[64,512]{1,0:T(8,128)(2,1)S(1)} %collective-permute-done.9.final_ref), custom_call_target="tpu_custom_call" | custom-call | flops 134217728 | bytes 1048576 | tf_op jit(solution)/shard_map/out/pallas_call | solution.py:351
  40.3 0.0 collective-permute-done.8.final_ref
  40.3 1.4 %out.3 = f32[128,1024]{1,0:T(8,128)} custom-call(bf16[128,512]{1,0:T(8,128)(2,1)S(1)} %get-tuple-element.30.refs_1_.q_ref, f32[128,512]{1,0:T(8,128)S(1)} %get-tuple-element.43.local_ref, f32[1,1024]{1,0:T(1,128)S(1)} %bitcast.6, bf16[1024,1024]{1,0:T(8,128)(2,1)S(1)} %copy-done.5, bf16[64,512]{1,0:T(8,128)(2,1)S(1)} %collective-permute-done.8.final_ref, ...), custom_call_target="tpu_custom_call" | custom-call | flops 134217728 | bytes 1048576 | tf_op jit(solution)/shard_map/out/pallas_call | solution.py:351
  (7 shorter events, 0.1 us)
Async XLA Ops:
  0.0 1.6 %copy-start = (bf16[1024,1024]{1,0:T(8,128)(2,1)S(1)}, bf16[1024,1024]{1,0:T(8,128)(2,1)}, u32[]{:S(2)}) copy-start(bf16[1024,1024]{1,0:T(8,128)(2,1)} %wk.1) | copy-start | bytes 6291460
  1.6 1.6 %copy-start.2 = (bf16[1024,1024]{1,0:T(8,128)(2,1)S(1)}, bf16[1024,1024]{1,0:T(8,128)(2,1)}, u32[]{:S(2)}) copy-start(bf16[1024,1024]{1,0:T(8,128)(2,1)} %wv.1) | copy-start | bytes 6291460
  3.2 0.9 %copy-start.6 = (bf16[128,1024]{1,0:T(8,128)(2,1)S(1)}, bf16[128,1024]{1,0:T(8,128)(2,1)}, u32[]{:S(2)}) copy-start(bf16[128,1024]{1,0:T(8,128)(2,1)} %x_ref.3) | copy-start | bytes 786436
  4.1 5.1 %copy-start.10 = (s32[1,4,4,2]{2,3,1,0:T(2,128)S(1)}, s32[1,4,4,2]{2,3,1,0:T(2,128)}, u32[]{:S(2)}) copy-start(s32[1,4,4,2]{2,3,1,0:T(2,128)} %param.9) | copy-start | bytes 388
  5.6 6.4 %collective-permute-start.3 = (bf16[64,1024]{1,0:T(8,128)(2,1)S(1)}, bf16[64,1024]{1,0:T(8,128)(2,1)S(1)}, u32[]{:S(2)}, u32[]{:S(2)}) collective-permute-start(bf16[64,1024]{1,0:T(8,128)(2,1)S(1)} %get-tuple-element.37), channel_id=1, source_target_pairs={{0,4},{4,0},{8,12},{12,8},{1,5},{5,1},{9,13},{13,9},{2,6},{6,2},{1... | collective-permute-start | bytes 393224 | tf_op jit(solution)/shard_map/ppermute | solution.py:190
  6.2 6.8 %collective-permute-start.4 = (bf16[64,1024]{1,0:T(8,128)(2,1)S(1)}, bf16[64,1024]{1,0:T(8,128)(2,1)S(1)}, u32[]{:S(2)}, u32[]{:S(2)}) collective-permute-start(bf16[64,1024]{1,0:T(8,128)(2,1)S(1)} %get-tuple-element.37), channel_id=1, source_target_pairs={{0,8},{4,12},{8,0},{12,4},{1,9},{5,13},{9,1},{13,5},{2,10},{6,14},... | collective-permute-start | bytes 393224 | tf_op jit(solution)/shard_map/ppermute | solution.py:190
  7.8 6.9 %collective-permute-start.5 = (bf16[64,1024]{1,0:T(8,128)(2,1)S(1)}, bf16[64,1024]{1,0:T(8,128)(2,1)S(1)}, u32[]{:S(2)}, u32[]{:S(2)}) collective-permute-start(bf16[64,1024]{1,0:T(8,128)(2,1)S(1)} %get-tuple-element.37), channel_id=1, source_target_pairs={{0,12},{4,8},{8,4},{12,0},{1,13},{5,9},{9,5},{13,1},{2,14},{6,10},... | collective-permute-start | bytes 393224 | tf_op jit(solution)/shard_map/ppermute | solution.py:190
  14.9 20.9 %copy-start.7 = (bf16[128,1024]{1,0:T(8,128)(2,1)S(1)}, bf16[128,1024]{1,0:T(8,128)(2,1)}, u32[]{:S(2)}) copy-start(bf16[128,1024]{1,0:T(8,128)(2,1)} %x_ref.3) | copy-start | bytes 786436
  14.9 20.9 %copy-start.8 = (s32[1,64,64]{2,1,0:T(8,128)S(1)}, s32[1,64,64]{2,1,0:T(8,128)}, u32[]{:S(2)}) copy-start(s32[1,64,64]{2,1,0:T(8,128)} %refs_0_.1) | copy-start | bytes 49156
  14.9 20.9 %copy-start.11 = (s32[1,4,4,2]{2,3,1,0:T(2,128)S(1)}, s32[1,4,4,2]{2,3,1,0:T(2,128)}, u32[]{:S(2)}) copy-start(s32[1,4,4,2]{2,3,1,0:T(2,128)} %param.9) | copy-start | bytes 388
  14.9 7.9 %collective-permute-start.7 = (bf16[1,64,1024]{2,1,0:T(8,128)(2,1)S(1)}, bf16[1,64,1024]{2,1,0:T(8,128)(2,1)S(1)}, u32[]{:S(2)}, u32[]{:S(2)}) collective-permute-start(bf16[1,64,1024]{2,1,0:T(8,128)(2,1)S(1)} %get-tuple-element.45), channel_id=1, source_target_pairs={{0,1},{1,0},{2,3},{3,2},{4,5},{5,4},{6,7},{7,6},{8,9},{9,8},{10,11... | collective-permute-start | bytes 393224 | tf_op jit(solution)/shard_map/ppermute | solution.py:190
  15.4 20.4 %copy-start.1 = (bf16[1024,1024]{1,0:T(8,128)(2,1)S(1)}, bf16[1024,1024]{1,0:T(8,128)(2,1)}, u32[]{:S(2)}) copy-start(bf16[1024,1024]{1,0:T(8,128)(2,1)} %wk.1) | copy-start | bytes 6291460
  15.4 20.4 %copy-start.3 = (bf16[1024,1024]{1,0:T(8,128)(2,1)S(1)}, bf16[1024,1024]{1,0:T(8,128)(2,1)}, u32[]{:S(2)}) copy-start(bf16[1024,1024]{1,0:T(8,128)(2,1)} %wv.1) | copy-start | bytes 6291460
  15.4 20.4 %copy-start.4 = (bf16[1024,1024]{1,0:T(8,128)(2,1)S(1)}, bf16[1024,1024]{1,0:T(8,128)(2,1)}, u32[]{:S(2)}) copy-start(bf16[1024,1024]{1,0:T(8,128)(2,1)} %refs_2_.3) | copy-start | bytes 6291460
  16.8 7.8 %collective-permute-start = (bf16[64,1024]{1,0:T(8,128)(2,1)S(1)}, bf16[64,1024]{1,0:T(8,128)(2,1)S(1)}, u32[]{:S(2)}, u32[]{:S(2)}) collective-permute-start(bf16[64,1024]{1,0:T(8,128)(2,1)S(1)} %get-tuple-element.26), channel_id=1, source_target_pairs={{0,1},{1,0},{2,3},{3,2},{4,5},{5,4},{6,7},{7,6},{8,9},{9,8},{10,11... | collective-permute-start | bytes 393224 | tf_op jit(solution)/shard_map/ppermute | solution.py:190
  18.4 11.7 %collective-permute-start.1 = (bf16[64,1024]{1,0:T(8,128)(2,1)S(1)}, bf16[64,1024]{1,0:T(8,128)(2,1)S(1)}, u32[]{:S(2)}, u32[]{:S(2)}) collective-permute-start(bf16[64,1024]{1,0:T(8,128)(2,1)S(1)} %get-tuple-element.27), channel_id=1, source_target_pairs={{0,2},{1,3},{2,0},{3,1},{4,6},{5,7},{6,4},{7,5},{8,10},{9,11},{10,... | collective-permute-start | bytes 393224 | tf_op jit(solution)/shard_map/ppermute | solution.py:190
  21.0 14.8 %collective-permute-start.2 = (bf16[64,1024]{1,0:T(8,128)(2,1)S(1)}, bf16[64,1024]{1,0:T(8,128)(2,1)S(1)}, u32[]{:S(2)}, u32[]{:S(2)}) collective-permute-start(bf16[64,1024]{1,0:T(8,128)(2,1)S(1)} %get-tuple-element.28), channel_id=1, source_target_pairs={{0,3},{1,2},{2,1},{3,0},{4,7},{5,6},{6,5},{7,4},{8,11},{9,10},{10,... | collective-permute-start | bytes 393224 | tf_op jit(solution)/shard_map/ppermute | solution.py:190
  21.0 18.3 %collective-permute-start.6 = (bf16[64,1024]{1,0:T(8,128)(2,1)S(1)}, bf16[64,1024]{1,0:T(8,128)(2,1)S(1)}, u32[]{:S(2)}, u32[]{:S(2)}) collective-permute-start(bf16[64,1024]{1,0:T(8,128)(2,1)S(1)} %get-tuple-element.42), channel_id=1, source_target_pairs={{0,1},{1,0},{2,3},{3,2},{4,5},{5,4},{6,7},{7,6},{8,9},{9,8},{10,11... | collective-permute-start | bytes 393224 | tf_op jit(solution)/shard_map/ppermute | solution.py:190
  22.9 16.8 %collective-permute-start.9 = (bf16[64,512]{1,0:T(8,128)(2,1)S(1)}, bf16[64,512]{1,0:T(8,128)(2,1)S(1)}, u32[]{:S(2)}, u32[]{:S(2)}) collective-permute-start(bf16[64,512]{1,0:T(8,128)(2,1)S(1)} %get-tuple-element.47), channel_id=1, source_target_pairs={{0,2},{1,3},{2,0},{3,1},{4,6},{5,7},{6,4},{7,5},{8,10},{9,11},{10,... | collective-permute-start | bytes 196616 | tf_op jit(solution)/shard_map/ppermute | solution.py:190
  24.6 15.7 %collective-permute-start.8 = (bf16[64,512]{1,0:T(8,128)(2,1)S(1)}, bf16[64,512]{1,0:T(8,128)(2,1)S(1)}, u32[]{:S(2)}, u32[]{:S(2)}) collective-permute-start(bf16[64,512]{1,0:T(8,128)(2,1)S(1)} %get-tuple-element.48), channel_id=1, source_target_pairs={{0,2},{1,3},{2,0},{3,1},{4,6},{5,7},{6,4},{7,5},{8,10},{9,11},{10,... | collective-permute-start | bytes 196616 | tf_op jit(solution)/shard_map/ppermute | solution.py:190
  38.0 1.7 %copy-start.5 = (bf16[1024,1024]{1,0:T(8,128)(2,1)S(1)}, bf16[1024,1024]{1,0:T(8,128)(2,1)}, u32[]{:S(2)}) copy-start(bf16[1024,1024]{1,0:T(8,128)(2,1)} %w.3) | copy-start | bytes 6291460
  38.0 1.7 %copy-start.9 = (f32[1024]{0:T(1024)S(1)}, f32[1024]{0:T(1024)}, u32[]{:S(2)}) copy-start(f32[1024]{0:T(1024)} %param.14) | copy-start | bytes 12292
